TPU v7x, 256 devices: a whole 4x4x8 slice. The times are simulated.
256 devices in a mesh: fu: 8 (over x, core), fv: 16 (over z, y_hi), ch: 2 (over y_lo).
Axes of the slice: x: 4, y: 4 (y_hi: 2, y_lo: 2; y = y_hi * 2 + y_lo), z: 8, core: 2. Of those that a mesh axis runs over, the one named last changes fastest.
Arguments:
- u_cell: int32 [8, 6144], P('fu', 'fv'), may hold values from 0 to 504, as said below
- v_cell: int32 [8, 6144], P('fu', 'fv'), may hold values from 0 to 2040, as said below
- w_plane: int32 [8, 6144], P('fu', 'fv'), may hold values from 0 to 15
- counts: int32 [8, 48], P('fu', 'fv'), may hold values from 1 to 128, 3840 in all within a row
- vis_values: bfloat16 [128, 8, 6144], P('ch', 'fu', 'fv'), may hold values from -6 to 6
- kern_u: float32 [16, 8], replicated, may hold values from 0.2 to 1
- kern_v: float32 [16, 8], replicated, may hold values from 0.2 to 1
Outputs:
- grid: float32 [128, 512, 2048], P('ch', 'fu', 'fv')
Inputs may be any that keep to these rules, and one draw needn't show every extreme that they name: Each row's u_cell lies in its own facet row's 64 cells, and the whole 8 by 8 support lies inside the grid. `v_cell`: the whole 8 by 8 support of each row lies inside the grid.
All inputs are finite; a program needn't handle non-finite values. No bound on the sum of `counts` on one device may be relied on, other than what follows from the above.
Results may differ from a plain program's by a relative error of at most 0.0039.
Values may be sent and summed in bfloat16 or wider, within the bound.
No kernel may reach another device: no remote copies, remote signals or barrier semaphores. Data moves between devices by JAX's collectives and lax.ppermute only.
A program may use at most 64 MiB of HBM per device.

v0:
```python
import jax
import jax.numpy as jnp
from jax import lax
from jax.sharding import PartitionSpec as P

GU = 64
GV = 128


def shifted(x, axis, by):
    length = lax.axis_size(axis)
    return lax.ppermute(x, axis, [(i, (i + by) % length) for i in range(length)])


def from_behind(block, axis, distance):
    devices = range(lax.axis_size(axis))
    route = [(i - distance, i) for i in devices if i - distance in devices]
    return lax.ppermute(block, axis, route)


def tap_matrix(weights, offsets, span):
    columns = jnp.arange(span, dtype=jnp.int32)
    result = jnp.zeros((weights.shape[0], span), jnp.float32)
    for shift_tap in range(weights.shape[1]):
        hit = (columns[None, :] == (offsets + shift_tap)[:, None]).astype(jnp.float32)
        result = result + weights[:, shift_tap : shift_tap + 1] * hit
    return result


def grid_rows(total, values, cells, base_u, base_v, kern_u, kern_v):
    planes = kern_u.shape[0]
    picker = (cells[2][:, None] == jnp.arange(planes, dtype=jnp.int32)[None, :]).astype(jnp.float32)
    weight_u = jnp.sum(picker[:, :, None] * kern_u[None, :, :], axis=1)
    weight_v = jnp.sum(picker[:, :, None] * kern_v[None, :, :], axis=1)
    off_u = cells[0] - base_u
    off_v = cells[1] - base_v
    keeper = (off_v >= 0) & (off_v < GV) & (off_u >= 0) & (off_u < GU) & (cells[3] > 0)
    weight_u = weight_u * keeper.astype(jnp.float32)[:, None]
    left = tap_matrix(weight_u, off_u, total.shape[1]).astype(jnp.bfloat16)
    right = tap_matrix(weight_v, off_v, total.shape[2])
    scaled = (values.astype(jnp.float32)[:, :, None] * right[None]).astype(jnp.bfloat16)
    return total + jnp.einsum("nu,cnv->cuv", left, scaled, preferred_element_type=jnp.float32)


def per_device(u_cell, v_cell, w_plane, counts, vis_values, kern_u, kern_v):
    rows = u_cell.shape[1]
    blocks = counts.shape[1]
    block_rows = rows // blocks
    position = jnp.arange(rows, dtype=jnp.int32)
    live = (position % block_rows < jnp.repeat(counts[0], block_rows)).astype(jnp.int32)
    cells = jnp.stack([u_cell[0], v_cell[0], w_plane[0], live])
    values = vis_values[:, 0, :]
    base_u = lax.axis_index("fu") * GU
    base_v = lax.axis_index("fv") * GV
    total = jnp.zeros((values.shape[0], GU + 8, GV + 8), jnp.float32)
    total = grid_rows(total, values, cells, base_u, base_v, kern_u, kern_v)

    def turn(step, state):
        acc, moving_values, moving_cells = state
        moving_values, moving_cells = shifted((moving_values, moving_cells), "fv", 1)
        acc = grid_rows(acc, moving_values, moving_cells, base_u, base_v, kern_u, kern_v)
        return (acc, moving_values, moving_cells)

    total, values, cells = lax.fori_loop(0, lax.axis_size("fv") - 1, turn, (total, values, cells))
    columns_in = from_behind(total[:, :, GV:], "fv", 1)
    merged = total[:, :, :GV].at[:, :, :8].add(columns_in)
    rows_in = from_behind(merged[:, GU:, :], "fu", 1)
    result = merged[:, :GU, :].at[:, :8, :].add(rows_in)
    return result


def solution(mesh):
    return jax.shard_map(
        per_device,
        mesh=mesh,
        in_specs=(
            P("fu", "fv"),
            P("fu", "fv"),
            P("fu", "fv"),
            P("fu", "fv"),
            P("ch", "fu", "fv"),
            P(),
            P(),
        ),
        out_specs=P("ch", "fu", "fv"),
        check_vma=False,
    )
```

profile of v0, /device:TPU:1, one launch (start us, length us, event | category | flops | bytes accessed | tf_op | source)
XLA Modules:
  0.0 276.7 jit_solution(11880258586147800881)
XLA Ops:
  6.4 4.7 %fusion.29 = f32[64,72,136]{1,2,0:T(8,128)} fusion(f32[384,136]{0,1:T(8,128)S(1)} %select_add_fusion.1, f32[64,384]{1,0:T(8,128)S(1)} %bitcast_convert_fusion, f32[384]{0:T(512)S(1)} %get-tuple-element.104, s32[384]{0:T(512)S(1)} %get-tuple-element.155, f32[384]{0:T(512)S(1)} %get-tuple-element.105, s32[384]{0:T(512)S(1)} %get-tuple-element.150, ...), kind=kOutput, calls=%fused_computation.88 | convolution fusion | flops 488644608 | bytes 2838528 | tf_op jit(solution)/shard_map/nu,cnv->cuv/dot_general | solution.py:42
  11.1 215.0 %while.16 = (s32[]{:T(128)}, f32[64,72,136]{1,2,0:T(8,128)}, bf16[64,384]{1,0:T(8,128)(2,1)S(1)}, s32[4,384]{1,0:T(4,128)S(1)}, s32[]{:T(128)}, /*index=5*/f32[1...) while((s32[]{:T(128)}, f32[64,72,136]{1,2,0:T(8,128)}, bf16[64,384]{1,0:T(8,128)(2,1)S(1)}, ...), condition=%wide.region_5.6_spmd, body=%wide.region_2.5_spmd.sunk | while | flops 490712832 | bytes 6250421 | solution.py:64
  11.1 3.7 %collective-permute-start = (s32[4,384]{1,0:T(4,128)S(1)}, s32[4,384]{1,0:T(4,128)S(1)}, u32[]{:S(2)}, u32[]{:S(2)}) collective-permute-start(s32[4,384]{1,0:T(4,128)S(1)} %get-tuple-element.296), channel_id=1, source_target_pairs={{0,2},{2,4},{4,6},{6,8},{8,10},{10,12},{12,14},{14,16},{16,18},{18... | collective-permute-start | bytes 18440 | tf_op jit(solution)/shard_map/while/body/eval_jaxpr/ppermute | solution.py:12
  16.2 4.9 %collective-permute-done = s32[4,384]{1,0:T(4,128)S(1)} collective-permute-done((s32[4,384]{1,0:T(4,128)S(1)}, s32[4,384]{1,0:T(4,128)S(1)}, u32[]{:S(2)}, u32[]{:S(2)}) %collective-permute-start) | collective-permute-done | bytes 6176 | tf_op jit(solution)/shard_map/while/body/eval_jaxpr/ppermute | solution.py:12
  21.7 7.0 %bitcast_add_fusion.2 = f32[64,72,136]{1,2,0:T(8,128)} fusion(f32[64,72,136]{1,2,0:T(8,128)} %get-tuple-element.294, f32[384,136]{0,1:T(8,128)S(1)} %select_add_fusion.3, f32[64,384]{1,0:T(8,128)S(1)} %convert_element_type.141, f32[384]{0:T(512)S(1)} %get-tuple-element.269, s32[384]{0:T(512)S(1)} %get-tuple-element.270, ...), kind=kOutput, calls=%fused_computation.4.clone.1 | convolution fusion | flops 489271296 | bytes 5345280 | tf_op jit(solution)/shard_map/while/body/eval_jaxpr/nu,cnv->cuv/dot_general | solution.py:42
  28.7 2.8 %collective-permute-start.1 = (bf16[64,384]{1,0:T(8,128)(2,1)S(1)}, bf16[64,384]{1,0:T(8,128)(2,1)S(1)}, u32[]{:S(2)}, u32[]{:S(2)}) collective-permute-start(bf16[64,384]{1,0:T(8,128)(2,1)S(1)} %get-tuple-element.295), channel_id=1, source_target_pairs={{0,2},{2,4},{4,6},{6,8},{8,10},{10,12},{12,14},{14,16},{16,18},{18... | collective-permute-start | bytes 147464 | tf_op jit(solution)/shard_map/while/body/eval_jaxpr/ppermute | solution.py:12
  31.5 3.3 %collective-permute-done = s32[4,384]{1,0:T(4,128)S(1)} collective-permute-done((s32[4,384]{1,0:T(4,128)S(1)}, s32[4,384]{1,0:T(4,128)S(1)}, u32[]{:S(2)}, u32[]{:S(2)}) %collective-permute-start) | collective-permute-done | bytes 6176 | tf_op jit(solution)/shard_map/while/body/eval_jaxpr/ppermute | solution.py:12
  35.3 7.0 %bitcast_add_fusion.2 = f32[64,72,136]{1,2,0:T(8,128)} fusion(f32[64,72,136]{1,2,0:T(8,128)} %get-tuple-element.294, f32[384,136]{0,1:T(8,128)S(1)} %select_add_fusion.3, f32[64,384]{1,0:T(8,128)S(1)} %convert_element_type.141, f32[384]{0:T(512)S(1)} %get-tuple-element.269, s32[384]{0:T(512)S(1)} %get-tuple-element.270, ...), kind=kOutput, calls=%fused_computation.4.clone.1 | convolution fusion | flops 489271296 | bytes 5345280 | tf_op jit(solution)/shard_map/while/body/eval_jaxpr/nu,cnv->cuv/dot_general | solution.py:42
  44.3 4.0 %collective-permute-done = s32[4,384]{1,0:T(4,128)S(1)} collective-permute-done((s32[4,384]{1,0:T(4,128)S(1)}, s32[4,384]{1,0:T(4,128)S(1)}, u32[]{:S(2)}, u32[]{:S(2)}) %collective-permute-start) | collective-permute-done | bytes 6176 | tf_op jit(solution)/shard_map/while/body/eval_jaxpr/ppermute | solution.py:12
  49.5 7.0 %bitcast_add_fusion.2 = f32[64,72,136]{1,2,0:T(8,128)} fusion(f32[64,72,136]{1,2,0:T(8,128)} %get-tuple-element.294, f32[384,136]{0,1:T(8,128)S(1)} %select_add_fusion.3, f32[64,384]{1,0:T(8,128)S(1)} %convert_element_type.141, f32[384]{0:T(512)S(1)} %get-tuple-element.269, s32[384]{0:T(512)S(1)} %get-tuple-element.270, ...), kind=kOutput, calls=%fused_computation.4.clone.1 | convolution fusion | flops 489271296 | bytes 5345280 | tf_op jit(solution)/shard_map/while/body/eval_jaxpr/nu,cnv->cuv/dot_general | solution.py:42
  56.5 3.1 %collective-permute-start.1 = (bf16[64,384]{1,0:T(8,128)(2,1)S(1)}, bf16[64,384]{1,0:T(8,128)(2,1)S(1)}, u32[]{:S(2)}, u32[]{:S(2)}) collective-permute-start(bf16[64,384]{1,0:T(8,128)(2,1)S(1)} %get-tuple-element.295), channel_id=1, source_target_pairs={{0,2},{2,4},{4,6},{6,8},{8,10},{10,12},{12,14},{14,16},{16,18},{18... | collective-permute-start | bytes 147464 | tf_op jit(solution)/shard_map/while/body/eval_jaxpr/ppermute | solution.py:12
  59.6 3.0 %collective-permute-done = s32[4,384]{1,0:T(4,128)S(1)} collective-permute-done((s32[4,384]{1,0:T(4,128)S(1)}, s32[4,384]{1,0:T(4,128)S(1)}, u32[]{:S(2)}, u32[]{:S(2)}) %collective-permute-start) | collective-permute-done | bytes 6176 | tf_op jit(solution)/shard_map/while/body/eval_jaxpr/ppermute | solution.py:12
  63.2 7.0 %bitcast_add_fusion.2 = f32[64,72,136]{1,2,0:T(8,128)} fusion(f32[64,72,136]{1,2,0:T(8,128)} %get-tuple-element.294, f32[384,136]{0,1:T(8,128)S(1)} %select_add_fusion.3, f32[64,384]{1,0:T(8,128)S(1)} %convert_element_type.141, f32[384]{0:T(512)S(1)} %get-tuple-element.269, s32[384]{0:T(512)S(1)} %get-tuple-element.270, ...), kind=kOutput, calls=%fused_computation.4.clone.1 | convolution fusion | flops 489271296 | bytes 5345280 | tf_op jit(solution)/shard_map/while/body/eval_jaxpr/nu,cnv->cuv/dot_general | solution.py:42
  72.5 3.8 %collective-permute-done = s32[4,384]{1,0:T(4,128)S(1)} collective-permute-done((s32[4,384]{1,0:T(4,128)S(1)}, s32[4,384]{1,0:T(4,128)S(1)}, u32[]{:S(2)}, u32[]{:S(2)}) %collective-permute-start) | collective-permute-done | bytes 6176 | tf_op jit(solution)/shard_map/while/body/eval_jaxpr/ppermute | solution.py:12
  77.6 7.0 %bitcast_add_fusion.2 = f32[64,72,136]{1,2,0:T(8,128)} fusion(f32[64,72,136]{1,2,0:T(8,128)} %get-tuple-element.294, f32[384,136]{0,1:T(8,128)S(1)} %select_add_fusion.3, f32[64,384]{1,0:T(8,128)S(1)} %convert_element_type.141, f32[384]{0:T(512)S(1)} %get-tuple-element.269, s32[384]{0:T(512)S(1)} %get-tuple-element.270, ...), kind=kOutput, calls=%fused_computation.4.clone.1 | convolution fusion | flops 489271296 | bytes 5345280 | tf_op jit(solution)/shard_map/while/body/eval_jaxpr/nu,cnv->cuv/dot_general | solution.py:42
  84.6 3.1 %collective-permute-start.1 = (bf16[64,384]{1,0:T(8,128)(2,1)S(1)}, bf16[64,384]{1,0:T(8,128)(2,1)S(1)}, u32[]{:S(2)}, u32[]{:S(2)}) collective-permute-start(bf16[64,384]{1,0:T(8,128)(2,1)S(1)} %get-tuple-element.295), channel_id=1, source_target_pairs={{0,2},{2,4},{4,6},{6,8},{8,10},{10,12},{12,14},{14,16},{16,18},{18... | collective-permute-start | bytes 147464 | tf_op jit(solution)/shard_map/while/body/eval_jaxpr/ppermute | solution.py:12
  87.7 3.0 %collective-permute-done = s32[4,384]{1,0:T(4,128)S(1)} collective-permute-done((s32[4,384]{1,0:T(4,128)S(1)}, s32[4,384]{1,0:T(4,128)S(1)}, u32[]{:S(2)}, u32[]{:S(2)}) %collective-permute-start) | collective-permute-done | bytes 6176 | tf_op jit(solution)/shard_map/while/body/eval_jaxpr/ppermute | solution.py:12
  91.3 7.0 %bitcast_add_fusion.2 = f32[64,72,136]{1,2,0:T(8,128)} fusion(f32[64,72,136]{1,2,0:T(8,128)} %get-tuple-element.294, f32[384,136]{0,1:T(8,128)S(1)} %select_add_fusion.3, f32[64,384]{1,0:T(8,128)S(1)} %convert_element_type.141, f32[384]{0:T(512)S(1)} %get-tuple-element.269, s32[384]{0:T(512)S(1)} %get-tuple-element.270, ...), kind=kOutput, calls=%fused_computation.4.clone.1 | convolution fusion | flops 489271296 | bytes 5345280 | tf_op jit(solution)/shard_map/while/body/eval_jaxpr/nu,cnv->cuv/dot_general | solution.py:42
  99.1 3.8 %collective-permute-start.1 = (bf16[64,384]{1,0:T(8,128)(2,1)S(1)}, bf16[64,384]{1,0:T(8,128)(2,1)S(1)}, u32[]{:S(2)}, u32[]{:S(2)}) collective-permute-start(bf16[64,384]{1,0:T(8,128)(2,1)S(1)} %get-tuple-element.295), channel_id=1, source_target_pairs={{0,2},{2,4},{4,6},{6,8},{8,10},{10,12},{12,14},{14,16},{16,18},{18... | collective-permute-start | bytes 147464 | tf_op jit(solution)/shard_map/while/body/eval_jaxpr/ppermute | solution.py:12
  105.7 7.0 %bitcast_add_fusion.2 = f32[64,72,136]{1,2,0:T(8,128)} fusion(f32[64,72,136]{1,2,0:T(8,128)} %get-tuple-element.294, f32[384,136]{0,1:T(8,128)S(1)} %select_add_fusion.3, f32[64,384]{1,0:T(8,128)S(1)} %convert_element_type.141, f32[384]{0:T(512)S(1)} %get-tuple-element.269, s32[384]{0:T(512)S(1)} %get-tuple-element.270, ...), kind=kOutput, calls=%fused_computation.4.clone.1 | convolution fusion | flops 489271296 | bytes 5345280 | tf_op jit(solution)/shard_map/while/body/eval_jaxpr/nu,cnv->cuv/dot_general | solution.py:42
  114.4 4.1 %collective-permute-start.1 = (bf16[64,384]{1,0:T(8,128)(2,1)S(1)}, bf16[64,384]{1,0:T(8,128)(2,1)S(1)}, u32[]{:S(2)}, u32[]{:S(2)}) collective-permute-start(bf16[64,384]{1,0:T(8,128)(2,1)S(1)} %get-tuple-element.295), channel_id=1, source_target_pairs={{0,2},{2,4},{4,6},{6,8},{8,10},{10,12},{12,14},{14,16},{16,18},{18... | collective-permute-start | bytes 147464 | tf_op jit(solution)/shard_map/while/body/eval_jaxpr/ppermute | solution.py:12
  121.0 7.0 %bitcast_add_fusion.2 = f32[64,72,136]{1,2,0:T(8,128)} fusion(f32[64,72,136]{1,2,0:T(8,128)} %get-tuple-element.294, f32[384,136]{0,1:T(8,128)S(1)} %select_add_fusion.3, f32[64,384]{1,0:T(8,128)S(1)} %convert_element_type.141, f32[384]{0:T(512)S(1)} %get-tuple-element.269, s32[384]{0:T(512)S(1)} %get-tuple-element.270, ...), kind=kOutput, calls=%fused_computation.4.clone.1 | convolution fusion | flops 489271296 | bytes 5345280 | tf_op jit(solution)/shard_map/while/body/eval_jaxpr/nu,cnv->cuv/dot_general | solution.py:42
  128.0 2.0 collective-permute-start
  130.0 1.9 collective-permute-start.1
  131.9 2.2 collective-permute-done
  134.6 1.9 collective-permute-done.1
  136.5 7.0 %bitcast_add_fusion.2 = f32[64,72,136]{1,2,0:T(8,128)} fusion(f32[64,72,136]{1,2,0:T(8,128)} %get-tuple-element.294, f32[384,136]{0,1:T(8,128)S(1)} %select_add_fusion.3, f32[64,384]{1,0:T(8,128)S(1)} %convert_element_type.141, f32[384]{0:T(512)S(1)} %get-tuple-element.269, s32[384]{0:T(512)S(1)} %get-tuple-element.270, ...), kind=kOutput, calls=%fused_computation.4.clone.1 | convolution fusion | flops 489271296 | bytes 5345280 | tf_op jit(solution)/shard_map/while/body/eval_jaxpr/nu,cnv->cuv/dot_general | solution.py:42
  143.5 2.0 collective-permute-start.1
  145.5 4.1 %collective-permute-done = s32[4,384]{1,0:T(4,128)S(1)} collective-permute-done((s32[4,384]{1,0:T(4,128)S(1)}, s32[4,384]{1,0:T(4,128)S(1)}, u32[]{:S(2)}, u32[]{:S(2)}) %collective-permute-start) | collective-permute-done | bytes 6176 | tf_op jit(solution)/shard_map/while/body/eval_jaxpr/ppermute | solution.py:12
  150.2 7.0 %bitcast_add_fusion.2 = f32[64,72,136]{1,2,0:T(8,128)} fusion(f32[64,72,136]{1,2,0:T(8,128)} %get-tuple-element.294, f32[384,136]{0,1:T(8,128)S(1)} %select_add_fusion.3, f32[64,384]{1,0:T(8,128)S(1)} %convert_element_type.141, f32[384]{0:T(512)S(1)} %get-tuple-element.269, s32[384]{0:T(512)S(1)} %get-tuple-element.270, ...), kind=kOutput, calls=%fused_computation.4.clone.1 | convolution fusion | flops 489271296 | bytes 5345280 | tf_op jit(solution)/shard_map/while/body/eval_jaxpr/nu,cnv->cuv/dot_general | solution.py:42
  157.2 2.0 collective-permute-start.1
  159.1 4.1 %collective-permute-done = s32[4,384]{1,0:T(4,128)S(1)} collective-permute-done((s32[4,384]{1,0:T(4,128)S(1)}, s32[4,384]{1,0:T(4,128)S(1)}, u32[]{:S(2)}, u32[]{:S(2)}) %collective-permute-start) | collective-permute-done | bytes 6176 | tf_op jit(solution)/shard_map/while/body/eval_jaxpr/ppermute | solution.py:12
  164.5 7.0 %bitcast_add_fusion.2 = f32[64,72,136]{1,2,0:T(8,128)} fusion(f32[64,72,136]{1,2,0:T(8,128)} %get-tuple-element.294, f32[384,136]{0,1:T(8,128)S(1)} %select_add_fusion.3, f32[64,384]{1,0:T(8,128)S(1)} %convert_element_type.141, f32[384]{0:T(512)S(1)} %get-tuple-element.269, s32[384]{0:T(512)S(1)} %get-tuple-element.270, ...), kind=kOutput, calls=%fused_computation.4.clone.1 | convolution fusion | flops 489271296 | bytes 5345280 | tf_op jit(solution)/shard_map/while/body/eval_jaxpr/nu,cnv->cuv/dot_general | solution.py:42
  171.5 1.8 collective-permute-start.1
  173.3 4.3 %collective-permute-done = s32[4,384]{1,0:T(4,128)S(1)} collective-permute-done((s32[4,384]{1,0:T(4,128)S(1)}, s32[4,384]{1,0:T(4,128)S(1)}, u32[]{:S(2)}, u32[]{:S(2)}) %collective-permute-start) | collective-permute-done | bytes 6176 | tf_op jit(solution)/shard_map/while/body/eval_jaxpr/ppermute | solution.py:12
  178.2 7.0 %bitcast_add_fusion.2 = f32[64,72,136]{1,2,0:T(8,128)} fusion(f32[64,72,136]{1,2,0:T(8,128)} %get-tuple-element.294, f32[384,136]{0,1:T(8,128)S(1)} %select_add_fusion.3, f32[64,384]{1,0:T(8,128)S(1)} %convert_element_type.141, f32[384]{0:T(512)S(1)} %get-tuple-element.269, s32[384]{0:T(512)S(1)} %get-tuple-element.270, ...), kind=kOutput, calls=%fused_computation.4.clone.1 | convolution fusion | flops 489271296 | bytes 5345280 | tf_op jit(solution)/shard_map/while/body/eval_jaxpr/nu,cnv->cuv/dot_general | solution.py:42
  186.6 4.6 %collective-permute-done = s32[4,384]{1,0:T(4,128)S(1)} collective-permute-done((s32[4,384]{1,0:T(4,128)S(1)}, s32[4,384]{1,0:T(4,128)S(1)}, u32[]{:S(2)}, u32[]{:S(2)}) %collective-permute-start) | collective-permute-done | bytes 6176 | tf_op jit(solution)/shard_map/while/body/eval_jaxpr/ppermute | solution.py:12
  191.8 7.0 %bitcast_add_fusion.2 = f32[64,72,136]{1,2,0:T(8,128)} fusion(f32[64,72,136]{1,2,0:T(8,128)} %get-tuple-element.294, f32[384,136]{0,1:T(8,128)S(1)} %select_add_fusion.3, f32[64,384]{1,0:T(8,128)S(1)} %convert_element_type.141, f32[384]{0:T(512)S(1)} %get-tuple-element.269, s32[384]{0:T(512)S(1)} %get-tuple-element.270, ...), kind=kOutput, calls=%fused_computation.4.clone.1 | convolution fusion | flops 489271296 | bytes 5345280 | tf_op jit(solution)/shard_map/while/body/eval_jaxpr/nu,cnv->cuv/dot_general | solution.py:42
  198.8 1.9 collective-permute-start.1
  200.7 4.2 %collective-permute-done = s32[4,384]{1,0:T(4,128)S(1)} collective-permute-done((s32[4,384]{1,0:T(4,128)S(1)}, s32[4,384]{1,0:T(4,128)S(1)}, u32[]{:S(2)}, u32[]{:S(2)}) %collective-permute-start) | collective-permute-done | bytes 6176 | tf_op jit(solution)/shard_map/while/body/eval_jaxpr/ppermute | solution.py:12
  205.5 7.0 %bitcast_add_fusion.2 = f32[64,72,136]{1,2,0:T(8,128)} fusion(f32[64,72,136]{1,2,0:T(8,128)} %get-tuple-element.294, f32[384,136]{0,1:T(8,128)S(1)} %select_add_fusion.3, f32[64,384]{1,0:T(8,128)S(1)} %convert_element_type.141, f32[384]{0:T(512)S(1)} %get-tuple-element.269, s32[384]{0:T(512)S(1)} %get-tuple-element.270, ...), kind=kOutput, calls=%fused_computation.4.clone.1 | convolution fusion | flops 489271296 | bytes 5345280 | tf_op jit(solution)/shard_map/while/body/eval_jaxpr/nu,cnv->cuv/dot_general | solution.py:42
  212.5 2.0 collective-permute-start.1
  214.5 4.1 %collective-permute-done = s32[4,384]{1,0:T(4,128)S(1)} collective-permute-done((s32[4,384]{1,0:T(4,128)S(1)}, s32[4,384]{1,0:T(4,128)S(1)}, u32[]{:S(2)}, u32[]{:S(2)}) %collective-permute-start) | collective-permute-done | bytes 6176 | tf_op jit(solution)/shard_map/while/body/eval_jaxpr/ppermute | solution.py:12
  219.1 7.0 %bitcast_add_fusion.2 = f32[64,72,136]{1,2,0:T(8,128)} fusion(f32[64,72,136]{1,2,0:T(8,128)} %get-tuple-element.294, f32[384,136]{0,1:T(8,128)S(1)} %select_add_fusion.3, f32[64,384]{1,0:T(8,128)S(1)} %convert_element_type.141, f32[384]{0:T(512)S(1)} %get-tuple-element.269, s32[384]{0:T(512)S(1)} %get-tuple-element.270, ...), kind=kOutput, calls=%fused_computation.4.clone.1 | convolution fusion | flops 489271296 | bytes 5345280 | tf_op jit(solution)/shard_map/while/body/eval_jaxpr/nu,cnv->cuv/dot_general | solution.py:42
  228.8 6.1 %copy.32 = f32[64,72,136]{2,1,0:T(8,128)} copy(f32[64,72,136]{1,2,0:T(8,128)} %get-tuple-element.71) | data formatting | bytes 5013504 | tf_op jit(solution)/shard_map/while | solution.py:64
  236.0 2.1 copy.33
  238.2 9.9 %scatter-add.6 = f32[64,72,128]{2,1,0:T(8,128)S(1)} dynamic-update-slice(f32[64,72,128]{2,1,0:T(8,128)S(1)} %slice-done, f32[64,72,8]{2,1,0:T(8,128)} %copy.33, s32[]{:T(128)} %constant.145.clone.1, s32[]{:T(128)} %constant.145.clone.1, s32[]{:T(128)} %constant.145.clone.1) | dynamic-update-slice | bytes 294916 | tf_op jit(solution)/shard_map/scatter-add | solution.py:66
  248.1 24.5 %collective-permute-start.3 = (f32[64,8,128]{2,1,0:T(8,128)S(1)}, f32[64,8,128]{2,1,0:T(8,128)S(1)}, u32[]{:S(2)}, u32[]{:S(2)}) collective-permute-start(f32[64,8,128]{2,1,0:T(8,128)S(1)} %slice.231), channel_id=1, source_target_pairs={{0,32},{32,64},{64,96},{96,128},{128,160},{160,192},{192,224},{1,3... | collective-permute-start | bytes 786440 | tf_op jit(solution)/shard_map/ppermute | solution.py:18
  (271 shorter events, 37.8 us)
Async XLA Ops:
  11.1 10.1 %collective-permute-start = (s32[4,384]{1,0:T(4,128)S(1)}, s32[4,384]{1,0:T(4,128)S(1)}, u32[]{:S(2)}, u32[]{:S(2)}) collective-permute-start(s32[4,384]{1,0:T(4,128)S(1)} %get-tuple-element.296), channel_id=1, source_target_pairs={{0,2},{2,4},{4,6},{6,8},{8,10},{10,12},{12,14},{14,16},{16,18},{18... | collective-permute-start | bytes 18440 | tf_op jit(solution)/shard_map/while/body/eval_jaxpr/ppermute | solution.py:12
  14.8 6.8 %collective-permute-start.1 = (bf16[64,384]{1,0:T(8,128)(2,1)S(1)}, bf16[64,384]{1,0:T(8,128)(2,1)S(1)}, u32[]{:S(2)}, u32[]{:S(2)}) collective-permute-start(bf16[64,384]{1,0:T(8,128)(2,1)S(1)} %get-tuple-element.295), channel_id=1, source_target_pairs={{0,2},{2,4},{4,6},{6,8},{8,10},{10,12},{12,14},{14,16},{16,18},{18... | collective-permute-start | bytes 147464 | tf_op jit(solution)/shard_map/while/body/eval_jaxpr/ppermute | solution.py:12
  28.7 6.1 %collective-permute-start = (s32[4,384]{1,0:T(4,128)S(1)}, s32[4,384]{1,0:T(4,128)S(1)}, u32[]{:S(2)}, u32[]{:S(2)}) collective-permute-start(s32[4,384]{1,0:T(4,128)S(1)} %get-tuple-element.296), channel_id=1, source_target_pairs={{0,2},{2,4},{4,6},{6,8},{8,10},{10,12},{12,14},{14,16},{16,18},{18... | collective-permute-start | bytes 18440 | tf_op jit(solution)/shard_map/while/body/eval_jaxpr/ppermute | solution.py:12
  28.7 6.6 %collective-permute-start.1 = (bf16[64,384]{1,0:T(8,128)(2,1)S(1)}, bf16[64,384]{1,0:T(8,128)(2,1)S(1)}, u32[]{:S(2)}, u32[]{:S(2)}) collective-permute-start(bf16[64,384]{1,0:T(8,128)(2,1)S(1)} %get-tuple-element.295), channel_id=1, source_target_pairs={{0,2},{2,4},{4,6},{6,8},{8,10},{10,12},{12,14},{14,16},{16,18},{18... | collective-permute-start | bytes 147464 | tf_op jit(solution)/shard_map/while/body/eval_jaxpr/ppermute | solution.py:12
  42.3 6.1 %collective-permute-start = (s32[4,384]{1,0:T(4,128)S(1)}, s32[4,384]{1,0:T(4,128)S(1)}, u32[]{:S(2)}, u32[]{:S(2)}) collective-permute-start(s32[4,384]{1,0:T(4,128)S(1)} %get-tuple-element.296), channel_id=1, source_target_pairs={{0,2},{2,4},{4,6},{6,8},{8,10},{10,12},{12,14},{14,16},{16,18},{18... | collective-permute-start | bytes 18440 | tf_op jit(solution)/shard_map/while/body/eval_jaxpr/ppermute | solution.py:12
  42.9 6.6 %collective-permute-start.1 = (bf16[64,384]{1,0:T(8,128)(2,1)S(1)}, bf16[64,384]{1,0:T(8,128)(2,1)S(1)}, u32[]{:S(2)}, u32[]{:S(2)}) collective-permute-start(bf16[64,384]{1,0:T(8,128)(2,1)S(1)} %get-tuple-element.295), channel_id=1, source_target_pairs={{0,2},{2,4},{4,6},{6,8},{8,10},{10,12},{12,14},{14,16},{16,18},{18... | collective-permute-start | bytes 147464 | tf_op jit(solution)/shard_map/while/body/eval_jaxpr/ppermute | solution.py:12
  56.5 6.1 %collective-permute-start = (s32[4,384]{1,0:T(4,128)S(1)}, s32[4,384]{1,0:T(4,128)S(1)}, u32[]{:S(2)}, u32[]{:S(2)}) collective-permute-start(s32[4,384]{1,0:T(4,128)S(1)} %get-tuple-element.296), channel_id=1, source_target_pairs={{0,2},{2,4},{4,6},{6,8},{8,10},{10,12},{12,14},{14,16},{16,18},{18... | collective-permute-start | bytes 18440 | tf_op jit(solution)/shard_map/while/body/eval_jaxpr/ppermute | solution.py:12
  56.5 6.6 %collective-permute-start.1 = (bf16[64,384]{1,0:T(8,128)(2,1)S(1)}, bf16[64,384]{1,0:T(8,128)(2,1)S(1)}, u32[]{:S(2)}, u32[]{:S(2)}) collective-permute-start(bf16[64,384]{1,0:T(8,128)(2,1)S(1)} %get-tuple-element.295), channel_id=1, source_target_pairs={{0,2},{2,4},{4,6},{6,8},{8,10},{10,12},{12,14},{14,16},{16,18},{18... | collective-permute-start | bytes 147464 | tf_op jit(solution)/shard_map/while/body/eval_jaxpr/ppermute | solution.py:12
  70.1 6.1 %collective-permute-start = (s32[4,384]{1,0:T(4,128)S(1)}, s32[4,384]{1,0:T(4,128)S(1)}, u32[]{:S(2)}, u32[]{:S(2)}) collective-permute-start(s32[4,384]{1,0:T(4,128)S(1)} %get-tuple-element.296), channel_id=1, source_target_pairs={{0,2},{2,4},{4,6},{6,8},{8,10},{10,12},{12,14},{14,16},{16,18},{18... | collective-permute-start | bytes 18440 | tf_op jit(solution)/shard_map/while/body/eval_jaxpr/ppermute | solution.py:12
  71.0 6.6 %collective-permute-start.1 = (bf16[64,384]{1,0:T(8,128)(2,1)S(1)}, bf16[64,384]{1,0:T(8,128)(2,1)S(1)}, u32[]{:S(2)}, u32[]{:S(2)}) collective-permute-start(bf16[64,384]{1,0:T(8,128)(2,1)S(1)} %get-tuple-element.295), channel_id=1, source_target_pairs={{0,2},{2,4},{4,6},{6,8},{8,10},{10,12},{12,14},{14,16},{16,18},{18... | collective-permute-start | bytes 147464 | tf_op jit(solution)/shard_map/while/body/eval_jaxpr/ppermute | solution.py:12
  84.6 6.1 %collective-permute-start = (s32[4,384]{1,0:T(4,128)S(1)}, s32[4,384]{1,0:T(4,128)S(1)}, u32[]{:S(2)}, u32[]{:S(2)}) collective-permute-start(s32[4,384]{1,0:T(4,128)S(1)} %get-tuple-element.296), channel_id=1, source_target_pairs={{0,2},{2,4},{4,6},{6,8},{8,10},{10,12},{12,14},{14,16},{16,18},{18... | collective-permute-start | bytes 18440 | tf_op jit(solution)/shard_map/while/body/eval_jaxpr/ppermute | solution.py:12
  84.6 6.6 %collective-permute-start.1 = (bf16[64,384]{1,0:T(8,128)(2,1)S(1)}, bf16[64,384]{1,0:T(8,128)(2,1)S(1)}, u32[]{:S(2)}, u32[]{:S(2)}) collective-permute-start(bf16[64,384]{1,0:T(8,128)(2,1)S(1)} %get-tuple-element.295), channel_id=1, source_target_pairs={{0,2},{2,4},{4,6},{6,8},{8,10},{10,12},{12,14},{14,16},{16,18},{18... | collective-permute-start | bytes 147464 | tf_op jit(solution)/shard_map/while/body/eval_jaxpr/ppermute | solution.py:12
  98.2 6.1 %collective-permute-start = (s32[4,384]{1,0:T(4,128)S(1)}, s32[4,384]{1,0:T(4,128)S(1)}, u32[]{:S(2)}, u32[]{:S(2)}) collective-permute-start(s32[4,384]{1,0:T(4,128)S(1)} %get-tuple-element.296), channel_id=1, source_target_pairs={{0,2},{2,4},{4,6},{6,8},{8,10},{10,12},{12,14},{14,16},{16,18},{18... | collective-permute-start | bytes 18440 | tf_op jit(solution)/shard_map/while/body/eval_jaxpr/ppermute | solution.py:12
  99.1 6.6 %collective-permute-start.1 = (bf16[64,384]{1,0:T(8,128)(2,1)S(1)}, bf16[64,384]{1,0:T(8,128)(2,1)S(1)}, u32[]{:S(2)}, u32[]{:S(2)}) collective-permute-start(bf16[64,384]{1,0:T(8,128)(2,1)S(1)} %get-tuple-element.295), channel_id=1, source_target_pairs={{0,2},{2,4},{4,6},{6,8},{8,10},{10,12},{12,14},{14,16},{16,18},{18... | collective-permute-start | bytes 147464 | tf_op jit(solution)/shard_map/while/body/eval_jaxpr/ppermute | solution.py:12
  112.7 6.1 %collective-permute-start = (s32[4,384]{1,0:T(4,128)S(1)}, s32[4,384]{1,0:T(4,128)S(1)}, u32[]{:S(2)}, u32[]{:S(2)}) collective-permute-start(s32[4,384]{1,0:T(4,128)S(1)} %get-tuple-element.296), channel_id=1, source_target_pairs={{0,2},{2,4},{4,6},{6,8},{8,10},{10,12},{12,14},{14,16},{16,18},{18... | collective-permute-start | bytes 18440 | tf_op jit(solution)/shard_map/while/body/eval_jaxpr/ppermute | solution.py:12
  114.4 6.6 %collective-permute-start.1 = (bf16[64,384]{1,0:T(8,128)(2,1)S(1)}, bf16[64,384]{1,0:T(8,128)(2,1)S(1)}, u32[]{:S(2)}, u32[]{:S(2)}) collective-permute-start(bf16[64,384]{1,0:T(8,128)(2,1)S(1)} %get-tuple-element.295), channel_id=1, source_target_pairs={{0,2},{2,4},{4,6},{6,8},{8,10},{10,12},{12,14},{14,16},{16,18},{18... | collective-permute-start | bytes 147464 | tf_op jit(solution)/shard_map/while/body/eval_jaxpr/ppermute | solution.py:12
  128.0 6.1 %collective-permute-start = (s32[4,384]{1,0:T(4,128)S(1)}, s32[4,384]{1,0:T(4,128)S(1)}, u32[]{:S(2)}, u32[]{:S(2)}) collective-permute-start(s32[4,384]{1,0:T(4,128)S(1)} %get-tuple-element.296), channel_id=1, source_target_pairs={{0,2},{2,4},{4,6},{6,8},{8,10},{10,12},{12,14},{14,16},{16,18},{18... | collective-permute-start | bytes 18440 | tf_op jit(solution)/shard_map/while/body/eval_jaxpr/ppermute | solution.py:12
  130.0 6.6 %collective-permute-start.1 = (bf16[64,384]{1,0:T(8,128)(2,1)S(1)}, bf16[64,384]{1,0:T(8,128)(2,1)S(1)}, u32[]{:S(2)}, u32[]{:S(2)}) collective-permute-start(bf16[64,384]{1,0:T(8,128)(2,1)S(1)} %get-tuple-element.295), channel_id=1, source_target_pairs={{0,2},{2,4},{4,6},{6,8},{8,10},{10,12},{12,14},{14,16},{16,18},{18... | collective-permute-start | bytes 147464 | tf_op jit(solution)/shard_map/while/body/eval_jaxpr/ppermute | solution.py:12
  143.5 6.1 %collective-permute-start = (s32[4,384]{1,0:T(4,128)S(1)}, s32[4,384]{1,0:T(4,128)S(1)}, u32[]{:S(2)}, u32[]{:S(2)}) collective-permute-start(s32[4,384]{1,0:T(4,128)S(1)} %get-tuple-element.296), channel_id=1, source_target_pairs={{0,2},{2,4},{4,6},{6,8},{8,10},{10,12},{12,14},{14,16},{16,18},{18... | collective-permute-start | bytes 18440 | tf_op jit(solution)/shard_map/while/body/eval_jaxpr/ppermute | solution.py:12
  143.5 6.6 %collective-permute-start.1 = (bf16[64,384]{1,0:T(8,128)(2,1)S(1)}, bf16[64,384]{1,0:T(8,128)(2,1)S(1)}, u32[]{:S(2)}, u32[]{:S(2)}) collective-permute-start(bf16[64,384]{1,0:T(8,128)(2,1)S(1)} %get-tuple-element.295), channel_id=1, source_target_pairs={{0,2},{2,4},{4,6},{6,8},{8,10},{10,12},{12,14},{14,16},{16,18},{18... | collective-permute-start | bytes 147464 | tf_op jit(solution)/shard_map/while/body/eval_jaxpr/ppermute | solution.py:12
  157.1 6.1 %collective-permute-start = (s32[4,384]{1,0:T(4,128)S(1)}, s32[4,384]{1,0:T(4,128)S(1)}, u32[]{:S(2)}, u32[]{:S(2)}) collective-permute-start(s32[4,384]{1,0:T(4,128)S(1)} %get-tuple-element.296), channel_id=1, source_target_pairs={{0,2},{2,4},{4,6},{6,8},{8,10},{10,12},{12,14},{14,16},{16,18},{18... | collective-permute-start | bytes 18440 | tf_op jit(solution)/shard_map/while/body/eval_jaxpr/ppermute | solution.py:12
  157.2 7.4 %collective-permute-start.1 = (bf16[64,384]{1,0:T(8,128)(2,1)S(1)}, bf16[64,384]{1,0:T(8,128)(2,1)S(1)}, u32[]{:S(2)}, u32[]{:S(2)}) collective-permute-start(bf16[64,384]{1,0:T(8,128)(2,1)S(1)} %get-tuple-element.295), channel_id=1, source_target_pairs={{0,2},{2,4},{4,6},{6,8},{8,10},{10,12},{12,14},{14,16},{16,18},{18... | collective-permute-start | bytes 147464 | tf_op jit(solution)/shard_map/while/body/eval_jaxpr/ppermute | solution.py:12
  171.5 6.1 %collective-permute-start = (s32[4,384]{1,0:T(4,128)S(1)}, s32[4,384]{1,0:T(4,128)S(1)}, u32[]{:S(2)}, u32[]{:S(2)}) collective-permute-start(s32[4,384]{1,0:T(4,128)S(1)} %get-tuple-element.296), channel_id=1, source_target_pairs={{0,2},{2,4},{4,6},{6,8},{8,10},{10,12},{12,14},{14,16},{16,18},{18... | collective-permute-start | bytes 18440 | tf_op jit(solution)/shard_map/while/body/eval_jaxpr/ppermute | solution.py:12
  171.5 6.6 %collective-permute-start.1 = (bf16[64,384]{1,0:T(8,128)(2,1)S(1)}, bf16[64,384]{1,0:T(8,128)(2,1)S(1)}, u32[]{:S(2)}, u32[]{:S(2)}) collective-permute-start(bf16[64,384]{1,0:T(8,128)(2,1)S(1)} %get-tuple-element.295), channel_id=1, source_target_pairs={{0,2},{2,4},{4,6},{6,8},{8,10},{10,12},{12,14},{14,16},{16,18},{18... | collective-permute-start | bytes 147464 | tf_op jit(solution)/shard_map/while/body/eval_jaxpr/ppermute | solution.py:12
  185.2 6.1 %collective-permute-start = (s32[4,384]{1,0:T(4,128)S(1)}, s32[4,384]{1,0:T(4,128)S(1)}, u32[]{:S(2)}, u32[]{:S(2)}) collective-permute-start(s32[4,384]{1,0:T(4,128)S(1)} %get-tuple-element.296), channel_id=1, source_target_pairs={{0,2},{2,4},{4,6},{6,8},{8,10},{10,12},{12,14},{14,16},{16,18},{18... | collective-permute-start | bytes 18440 | tf_op jit(solution)/shard_map/while/body/eval_jaxpr/ppermute | solution.py:12
  185.2 6.6 %collective-permute-start.1 = (bf16[64,384]{1,0:T(8,128)(2,1)S(1)}, bf16[64,384]{1,0:T(8,128)(2,1)S(1)}, u32[]{:S(2)}, u32[]{:S(2)}) collective-permute-start(bf16[64,384]{1,0:T(8,128)(2,1)S(1)} %get-tuple-element.295), channel_id=1, source_target_pairs={{0,2},{2,4},{4,6},{6,8},{8,10},{10,12},{12,14},{14,16},{16,18},{18... | collective-permute-start | bytes 147464 | tf_op jit(solution)/shard_map/while/body/eval_jaxpr/ppermute | solution.py:12
  198.8 6.1 %collective-permute-start = (s32[4,384]{1,0:T(4,128)S(1)}, s32[4,384]{1,0:T(4,128)S(1)}, u32[]{:S(2)}, u32[]{:S(2)}) collective-permute-start(s32[4,384]{1,0:T(4,128)S(1)} %get-tuple-element.296), channel_id=1, source_target_pairs={{0,2},{2,4},{4,6},{6,8},{8,10},{10,12},{12,14},{14,16},{16,18},{18... | collective-permute-start | bytes 18440 | tf_op jit(solution)/shard_map/while/body/eval_jaxpr/ppermute | solution.py:12
  198.8 6.6 %collective-permute-start.1 = (bf16[64,384]{1,0:T(8,128)(2,1)S(1)}, bf16[64,384]{1,0:T(8,128)(2,1)S(1)}, u32[]{:S(2)}, u32[]{:S(2)}) collective-permute-start(bf16[64,384]{1,0:T(8,128)(2,1)S(1)} %get-tuple-element.295), channel_id=1, source_target_pairs={{0,2},{2,4},{4,6},{6,8},{8,10},{10,12},{12,14},{14,16},{16,18},{18... | collective-permute-start | bytes 147464 | tf_op jit(solution)/shard_map/while/body/eval_jaxpr/ppermute | solution.py:12
  212.4 6.1 %collective-permute-start = (s32[4,384]{1,0:T(4,128)S(1)}, s32[4,384]{1,0:T(4,128)S(1)}, u32[]{:S(2)}, u32[]{:S(2)}) collective-permute-start(s32[4,384]{1,0:T(4,128)S(1)} %get-tuple-element.296), channel_id=1, source_target_pairs={{0,2},{2,4},{4,6},{6,8},{8,10},{10,12},{12,14},{14,16},{16,18},{18... | collective-permute-start | bytes 18440 | tf_op jit(solution)/shard_map/while/body/eval_jaxpr/ppermute | solution.py:12
  212.5 6.6 %collective-permute-start.1 = (bf16[64,384]{1,0:T(8,128)(2,1)S(1)}, bf16[64,384]{1,0:T(8,128)(2,1)S(1)}, u32[]{:S(2)}, u32[]{:S(2)}) collective-permute-start(bf16[64,384]{1,0:T(8,128)(2,1)S(1)} %get-tuple-element.295), channel_id=1, source_target_pairs={{0,2},{2,4},{4,6},{6,8},{8,10},{10,12},{12,14},{14,16},{16,18},{18... | collective-permute-start | bytes 147464 | tf_op jit(solution)/shard_map/while/body/eval_jaxpr/ppermute | solution.py:12
  227.1 7.8 %collective-permute-start.2 = (f32[64,72,8]{1,2,0:T(8,128)S(1)}, f32[64,72,8]{1,2,0:T(8,128)S(1)}, u32[]{:S(2)}, u32[]{:S(2)}) collective-permute-start(f32[64,72,8]{1,2,0:T(8,128)S(1)} %slice.188), channel_id=1, source_target_pairs={{0,2},{2,4},{4,6},{6,8},{8,10},{10,12},{12,14},{14,16},{16,18},{18... | collective-permute-start | bytes 442376 | tf_op jit(solution)/shard_map/ppermute | solution.py:18
  234.9 3.3 %slice-start = ((f32[64,72,136]{2,1,0:T(8,128)}), f32[64,72,128]{2,1,0:T(8,128)S(1)}, s32[]{:S(2)}) async-start(f32[64,72,136]{2,1,0:T(8,128)} %copy.32), calls=%async_computation | async-start | bytes 4718592 | tf_op jit(solution)/shard_map/slice | solution.py:66
  248.1 27.8 %collective-permute-start.3 = (f32[64,8,128]{2,1,0:T(8,128)S(1)}, f32[64,8,128]{2,1,0:T(8,128)S(1)}, u32[]{:S(2)}, u32[]{:S(2)}) collective-permute-start(f32[64,8,128]{2,1,0:T(8,128)S(1)} %slice.231), channel_id=1, source_target_pairs={{0,32},{32,64},{64,96},{96,128},{128,160},{160,192},{192,224},{1,3... | collective-permute-start | bytes 786440 | tf_op jit(solution)/shard_map/ppermute | solution.py:18
where the time goes:
time: 278 us; the launch traced here: 277 us
  matrix products  109 us (39%)
  starting transfers between devices  70.4 us (25%)
  waiting for transfers between devices  59.9 us (22%)
  local copies, waits for them, and re-layouts  25.4 us (9%)
  other arithmetic  10.5 us (4%)
    dot_general x16, matrix products, grid_rows(): jnp.einsum('nu,cnv->cuv', left, scaled, preferred_element_type=jnp.float32)  109 us
    ppermute x30, waiting for transfers between devices, shifted(): lax.ppermute(x, axis, [(i, (i + by) % length) for i in range(length)])  58.2 us
    ppermute x30, starting transfers between devices, shifted(): lax.ppermute(x, axis, [(i, (i + by) % length) for i in range(length)])  44.2 us
    ppermute x2, starting transfers between devices, from_behind(): return lax.ppermute(block, axis, route)  26.3 us
    scatter-add x1, local copies, waits for them, and re-layouts, per_device(): merged = total[:, :, :GV].at[:, :, :8].add(columns_in)  9.94 us
    while x1, local copies, waits for them, and re-layouts, per_device(): lax.fori_loop(0, lax.axis_size('fv') - 1, turn, (total, values, cells))  6.07 us
  transfers between devices with their start and end apart: 32, of which 22 were waited for; matrix products, arithmetic and copies ran while one was open for 5% of the time, Pallas kernels for 0%

commit v1 on v0

v1 whole, which is shorter than its diff:
```python
import functools

import jax
import jax.numpy as jnp
from jax import lax
from jax.experimental import pallas as pl
from jax.experimental.pallas import tpu as pltpu
from jax.sharding import PartitionSpec as P

GU = 64
GV = 128
TAPS = 8
LANES = 128
META = 8
KT = 256
F32 = jnp.float32
BF16 = jnp.bfloat16
NT = (((1,), (1,)), ((), ()))


def pack_kernel(cap, n_dst, u_ref, v_ref, w_ref, counts_ref, vis_ref, out_ref):
    chans, _, rows = vis_ref.shape
    n_blocks = counts_ref.shape[1]
    block = rows // n_blocks
    u, v, w = u_ref[...], v_ref[...], w_ref[...]
    lane = lax.broadcasted_iota(jnp.int32, (1, rows), 1)
    limit = jnp.zeros((1, rows), jnp.int32)
    for b in range(n_blocks):
        limit = jnp.where(lane >= b * block, b * block + counts_ref[0, b], limit)
    live = lane < limit
    first = v // GV
    last = (v + (TAPS - 1)) // GV
    dst = lax.broadcasted_iota(jnp.int32, (n_dst, rows), 0)
    member = ((dst == first) | (dst == last)) & live
    member_f = member.astype(F32)
    before = lax.broadcasted_iota(jnp.int32, (rows, rows), 0) < lax.broadcasted_iota(
        jnp.int32, (rows, rows), 1
    )
    rank = jnp.dot(
        member_f.astype(BF16),
        before.astype(F32).astype(BF16),
        preferred_element_type=F32,
    )
    rank = jnp.where(member, rank.astype(jnp.int32), -1)
    total = jnp.sum(member_f, axis=1, keepdims=True)
    over = (jnp.max(total, axis=0, keepdims=True) > cap).astype(F32)
    meta = jnp.concatenate(
        [
            (u % GU).astype(F32),
            (v % GV).astype(F32),
            first.astype(F32),
            w.astype(F32),
            jnp.zeros((META - 4, rows), F32),
        ],
        axis=0,
    ).astype(BF16)
    vis = vis_ref[:, 0, :]
    slot = lax.broadcasted_iota(jnp.int32, (cap, rows), 0)
    row_id = lax.broadcasted_iota(jnp.int32, (META, cap), 0)
    for d in range(n_dst):
        pick = (slot == rank[d : d + 1, :]).astype(F32).astype(BF16)
        sent = lax.dot_general(vis, pick, NT, preferred_element_type=F32)
        tags = lax.dot_general(meta, pick, NT, preferred_element_type=F32)
        held = jnp.minimum(total[d : d + 1, :], float(cap))
        tags = jnp.where(row_id == 4, over, tags)
        tags = jnp.where(row_id == 5, jnp.floor(held / 64.0), tags)
        tags = jnp.where(row_id == 6, held - 64.0 * jnp.floor(held / 64.0), tags)
        out_ref[d, :chans, :] = sent.astype(BF16)
        out_ref[d, chans:, :] = tags.astype(BF16)


def pack(cap, n_dst, u, v, w, counts, vis):
    chans = vis.shape[0]
    vmem = pl.BlockSpec(memory_space=pltpu.VMEM)
    return pl.pallas_call(
        functools.partial(pack_kernel, cap, n_dst),
        out_shape=jax.ShapeDtypeStruct((n_dst, chans + META, cap), BF16),
        in_specs=[vmem, vmem, vmem, pl.BlockSpec(memory_space=pltpu.SMEM), vmem],
        out_specs=vmem,
        compiler_params=pltpu.CompilerParams(vmem_limit_bytes=48 << 20),
    )(u, v, w, counts, vis)


def tap_rows(table, plane):
    result = jnp.zeros((TAPS, plane.shape[1]), F32)
    for p in range(table.shape[1]):
        result = jnp.where(plane == p, table[:, p : p + 1], result)
    return result


def spread(taps, start, low, span):
    cell = lax.broadcasted_iota(jnp.int32, (span, taps.shape[1]), 0) + (low - start)
    result = jnp.zeros((span, taps.shape[1]), F32)
    for t in range(TAPS):
        result = jnp.where(cell == t, taps[t : t + 1, :], result)
    return result


def v_weights(tags, plane, kern_v, facet):
    start = tags[1:2, :] + GV * (tags[2:3, :] - facet)
    wide = spread(tap_rows(kern_v, plane), start, 0, GV)
    high = wide.astype(BF16)
    low = (wide - high.astype(F32)).astype(BF16)
    return jnp.concatenate([high, low], axis=0)


def weighted(vis, ku):
    chans, span, lanes = vis.shape[0], ku.shape[0], vis.shape[1]
    full = vis[:, None, :] * ku[None, :, :]
    return full.reshape(chans * span, lanes).astype(BF16)


def border_kernel(msgs_ref, kern_u_ref, kern_v_ref, held_ref, tiles_ref, halo_ref, acc):
    n_src, depth, cap = msgs_ref.shape
    chans = depth - META
    facet = lax.axis_index("fv")
    parts = cap // LANES
    last_tile = held_ref.shape[1] // LANES - 1
    lane = lax.broadcasted_iota(jnp.int32, (depth, LANES), 1)

    def put(tile, value):
        at = pl.multiple_of(tile * LANES, LANES)
        held_ref[:, pl.ds(at, LANES)] = value.astype(BF16)

    def add_source(src, state):
        offset, tile = state
        tags = msgs_ref[src, chans:, :LANES].astype(F32)
        length = (64.0 * jnp.max(tags[5:6, :]) + jnp.max(tags[6:7, :])).astype(jnp.int32)
        for part in range(parts):
            block = msgs_ref[src, :, part * LANES : (part + 1) * LANES].astype(F32)
            shift = offset % LANES
            turned = pltpu.roll(block, shift, 1)
            at = offset // LANES
            put(at, jnp.where(lane < shift, tile, turned))
            spill = jnp.where(lane < shift, turned, 0.0)
            put(at + 1, spill)
            here = jnp.clip(length - part * LANES, 0, LANES)
            crossed = shift + here >= LANES
            tile = jnp.where(crossed, spill, jnp.where(lane < shift, tile, turned))
            offset = offset + here
        return offset, tile

    offset, _ = lax.fori_loop(0, n_src, add_source, (0, jnp.zeros((depth, LANES), F32)))
    put(jnp.minimum(offset // LANES + 1, last_tile), jnp.zeros((depth, LANES), F32))
    tiles = (offset + KT - 1) // KT
    tiles_ref[0, 0] = tiles
    acc[...] = jnp.zeros_like(acc)
    kern_u, kern_v = kern_u_ref[...].T, kern_v_ref[...].T

    def step(k, _):
        cols = pl.ds(pl.multiple_of(k * KT, KT), KT)
        vis = held_ref[:chans, cols].astype(F32)
        tags = held_ref[chans:, cols].astype(F32).astype(jnp.int32)
        plane = tags[3:4, :]
        ku = spread(tap_rows(kern_u, plane), tags[0:1, :], GU, TAPS)
        left = weighted(vis, ku.astype(BF16).astype(F32))
        right = v_weights(tags, plane, kern_v, facet)
        acc[...] += lax.dot_general(left, right, NT, preferred_element_type=F32)
        return 0

    lax.fori_loop(0, tiles, step, 0)
    halo_ref[...] = (acc[:, :GV] + acc[:, GV:]).reshape(chans, TAPS, GV).astype(BF16)


def border(msgs, kern_u, kern_v, width):
    n_src, depth, cap = msgs.shape
    chans = depth - META
    vmem = pl.BlockSpec(memory_space=pltpu.VMEM)
    return pl.pallas_call(
        border_kernel,
        out_shape=(
            jax.ShapeDtypeStruct((depth, width), BF16),
            jax.ShapeDtypeStruct((1, 1), jnp.int32),
            jax.ShapeDtypeStruct((chans, TAPS, GV), BF16),
        ),
        in_specs=[vmem] * 3,
        out_specs=(vmem, pl.BlockSpec(memory_space=pltpu.SMEM), vmem),
        scratch_shapes=[pltpu.VMEM((chans * TAPS, 2 * GV), F32)],
        compiler_params=pltpu.CompilerParams(vmem_limit_bytes=48 << 20),
    )(msgs, kern_u, kern_v)


def main_kernel(step_chans, tiles_ref, held_ref, kern_u_ref, kern_v_ref, out_ref, ku_s, kv_s, acc):
    chans = held_ref.shape[0] - META
    facet = lax.axis_index("fv")
    i = pl.program_id(0)
    tiles = tiles_ref[0, 0]

    @pl.when(i == 0)
    def _():
        kern_u, kern_v = kern_u_ref[...].T, kern_v_ref[...].T

        def prepare(k, _):
            cols = pl.ds(pl.multiple_of(k * KT, KT), KT)
            tags = held_ref[chans:, cols].astype(F32).astype(jnp.int32)
            plane = tags[3:4, :]
            ku_s[:, cols] = spread(tap_rows(kern_u, plane), tags[0:1, :], 0, GU).astype(BF16)
            kv_s[:, cols] = v_weights(tags, plane, kern_v, facet)
            return 0

        lax.fori_loop(0, tiles, prepare, 0)

    acc[...] = jnp.zeros_like(acc)
    first = pl.multiple_of(i * step_chans, step_chans)

    def step(k, _):
        cols = pl.ds(pl.multiple_of(k * KT, KT), KT)
        vis = held_ref[pl.ds(first, step_chans), cols].astype(F32)
        left = weighted(vis, ku_s[:, cols].astype(F32))
        acc[...] += lax.dot_general(left, kv_s[:, cols], NT, preferred_element_type=F32)
        return 0

    lax.fori_loop(0, tiles, step, 0)
    out_ref[...] = (acc[:, :GV] + acc[:, GV:]).reshape(step_chans, GU, GV)


def main(tiles, held, kern_u, kern_v, step_chans=8):
    depth, width = held.shape
    chans = depth - META
    vmem = pl.BlockSpec(memory_space=pltpu.VMEM)
    return pl.pallas_call(
        functools.partial(main_kernel, step_chans),
        grid=(chans // step_chans,),
        out_shape=jax.ShapeDtypeStruct((chans, GU, GV), F32),
        in_specs=[pl.BlockSpec(memory_space=pltpu.SMEM)] + [vmem] * 3,
        out_specs=pl.BlockSpec((step_chans, GU, GV), lambda i: (i, 0, 0)),
        scratch_shapes=[
            pltpu.VMEM((GU, width), BF16),
            pltpu.VMEM((2 * GV, width), BF16),
            pltpu.VMEM((step_chans * GU, 2 * GV), F32),
        ],
        compiler_params=pltpu.CompilerParams(
            dimension_semantics=("arbitrary",), vmem_limit_bytes=48 << 20
        ),
    )(tiles, held, kern_u, kern_v)


def join_kernel(grid_ref, halo_ref, out_ref):
    out_ref[...] = grid_ref[...] + halo_ref[...].astype(F32)


def join(grid, halo):
    chans = grid.shape[0]
    strip = pl.BlockSpec((chans, TAPS, GV), lambda i: (0, 0, 0))
    return pl.pallas_call(
        join_kernel,
        grid=(1,),
        out_shape=jax.ShapeDtypeStruct(grid.shape, grid.dtype),
        in_specs=[strip, strip],
        out_specs=strip,
        input_output_aliases={0: 0},
    )(grid, halo)


def per_device(u_cell, v_cell, w_plane, counts, vis_values, kern_u, kern_v):
    n_fv = lax.axis_size("fv")
    n_fu = lax.axis_size("fu")
    rows = u_cell.shape[1]
    chans = vis_values.shape[0]
    width = 4096
    small = 128

    def exchange(cap):
        sent = pack(cap, n_fv, u_cell, v_cell, w_plane, counts, vis_values)
        return lax.all_to_all(sent, "fv", 0, 0)

    msgs = exchange(small)
    over = jnp.max(msgs[:, chans + 4, 0]) > 0

    def whole():
        return border(exchange(rows), kern_u, kern_v, width)

    held, tiles, halo = lax.cond(over, whole, lambda: border(msgs, kern_u, kern_v, width))
    came = lax.ppermute(halo, "fu", [(i, i + 1) for i in range(n_fu - 1)])
    return join(main(tiles, held, kern_u, kern_v), came)


def solution(mesh):
    return jax.shard_map(
        per_device,
        mesh=mesh,
        in_specs=(
            P("fu", "fv"),
            P("fu", "fv"),
            P("fu", "fv"),
            P("fu", "fv"),
            P("ch", "fu", "fv"),
            P(),
            P(),
        ),
        out_specs=P("ch", "fu", "fv"),
        check_vma=False,
    )
```

time: 278 us -> 49.6 us (0.18)
  matrix products: 109 us -> 0 us
  starting transfers between devices: 70.4 us -> 17.1 us
  waiting for transfers between devices: 59.9 us -> 12.8 us
  local copies, waits for them, and re-layouts: 25.4 us -> 4.55 us
  Pallas kernels: 0 us -> 13.4 us
  other arithmetic: 10.5 us -> 0.62 us
    dot_general x16 -> x0, matrix products: 109 us -> none  [grid_rows(): jnp.einsum('nu,cnv->cuv', left, scaled, preferred_element_type=jnp.float32)]
    ppermute x32 -> x1, starting transfers between devices: 70.4 us -> 5.33 us  [per_device(): came = lax.ppermute(halo, 'fu', [(i, i + 1) for i in range(n_fu - 1)])]
    ppermute x32 -> x1, waiting for transfers between devices: 59.9 us -> 0.01 us  [per_device(): came = lax.ppermute(halo, 'fu', [(i, i + 1) for i in range(n_fu - 1)])]
    pallas_call x0 -> x4, Pallas kernels: none -> 13.4 us  [the longest x1 5.51 us: main(): pl.pallas_call(functools.partial(main_kernel, step_chans), grid=(chans //...]
    all_to_all x0 -> x1, waiting for transfers between devices: none -> 12.8 us  [exchange(): return lax.all_to_all(sent, 'fv', 0, 0)]
    all_to_all x0 -> x1, starting transfers between devices: none -> 11.7 us  [exchange(): return lax.all_to_all(sent, 'fv', 0, 0)]
    scatter-add x1 -> x0, local copies, waits for them, and re-layouts: 9.94 us -> none  [per_device(): merged = total[:, :, :GV].at[:, :, :8].add(columns_in)]
    while x31 -> x0, local copies, waits for them, and re-layouts: 6.2 us -> none  [the longest x1 6.07 us: per_device(): lax.fori_loop(0, lax.axis_size('fv') - 1, turn, (total, values, cells))]
  transfers between devices with their start and end apart: 32 -> 2, of which waited for: 22 -> 1; matrix products, arithmetic and copies ran while one was open for 5% -> 3% of each run, Pallas kernels for 0% -> 11%
where the time goes in v1:
time: 49.6 us; the launch traced here: 49.1 us
  starting transfers between devices  17.1 us (34%)
  Pallas kernels  13.4 us (27%)
  waiting for transfers between devices  12.8 us (26%)
  local copies, waits for them, and re-layouts  4.55 us (9%)
  between operations  0.69 us (1%)
  other arithmetic  0.62 us (1%)
    all_to_all x1, waiting for transfers between devices, exchange(): return lax.all_to_all(sent, 'fv', 0, 0)  12.8 us
    all_to_all x1, starting transfers between devices, exchange(): return lax.all_to_all(sent, 'fv', 0, 0)  11.7 us
    pallas_call x1, Pallas kernels, main(): pl.pallas_call(functools.partial(main_kernel, step_chans), grid=(chans //...  5.51 us
    ppermute x1, starting transfers between devices, per_device(): came = lax.ppermute(halo, 'fu', [(i, i + 1) for i in range(n_fu - 1)])  5.33 us
    pallas_call x1, Pallas kernels, border(): pl.pallas_call(border_kernel, out_shape=(jax.ShapeDtypeStruct((depth, wid...  3.1 us
    pallas_call x1, Pallas kernels, pack(): pl.pallas_call(functools.partial(pack_kernel, cap, n_dst), out_shape=jax....  3.06 us
    unnamed x5, local copies, waits for them, and re-layouts  3.04 us
    pallas_call x1, Pallas kernels, join(): pl.pallas_call(join_kernel, grid=(1,), out_shape=jax.ShapeDtypeStruct(gri...  1.71 us
  transfers between devices with their start and end apart: 2, of which 1 were waited for; matrix products, arithmetic and copies ran while one was open for 3% of the time, Pallas kernels for 11%

profile of v1, /device:TPU:1, one launch (start us, length us, event | category | flops | bytes accessed | tf_op | source)
XLA Modules:
  0.0 49.1 jit_solution(17992792257566023320)
XLA Ops:
  0.0 0.9 %copy.9.vis_ref = bf16[64,1,384]{2,1,0:T(2,128)(2,1)S(1)} copy(bf16[64,1,384]{2,0,1:T(8,128)(2,1)} %param.13) | data formatting | bytes 98304 | tf_op args[4]
  0.9 3.1 %shard_map.73 = bf16[16,72,128]{2,1,0:T(8,128)(2,1)} custom-call(s32[1,384]{1,0:T(1,128)} %u_ref.1, s32[1,384]{1,0:T(1,128)} %v_ref.1, s32[1,384]{1,0:T(1,128)} %w_ref.1, s32[1,3]{1,0:T(1,128)} %counts_ref.1, bf16[64,1,384]{2,1,0:T(2,128)(2,1)S(1)} %copy.9.vis_ref), custom_call_target="tpu_custom_call" | custom-call | tf_op jit(solution)/shard_map/pallas_call | solution.py:75
  3.9 11.7 %all-to-all-start.1 = ((bf16[16,72,128]{2,1,0:T(8,128)(2,1)}), bf16[16,72,128]{2,1,0:T(8,128)(2,1)S(1)}, u32[]{:S(2)}, u32[]{:S(2)}) async-start(bf16[16,72,128]{2,1,0:T(8,128)(2,1)} %shard_map.73), calls=%async_computation.1 | async-start | bytes 589824 | tf_op jit(solution)/shard_map/all_to_all | solution.py:265
  15.7 12.8 %all-to-all-done.1 = bf16[16,72,128]{2,1,0:T(8,128)(2,1)S(1)} async-done(((bf16[16,72,128]{2,1,0:T(8,128)(2,1)}), bf16[16,72,128]{2,1,0:T(8,128)(2,1)S(1)}, u32[]{:S(2)}, u32[]{:S(2)}) %all-to-all-start.1) | async-done | bytes 294944 | tf_op jit(solution)/shard_map/all_to_all | solution.py:265
  28.5 0.6 %slice_reduce_fusion = bf16[]{:T(256)} fusion(bf16[16,72,128]{2,1,0:T(8,128)(2,1)S(1)} %all-to-all-done.1), kind=kLoop, calls=%fused_computation | loop fusion | flops 15 | bytes 34 | tf_op jit(solution)/shard_map/reduce_max | solution.py:268
  29.7 4.6 %conditional.1 = ((bf16[72,4096]{1,0:T(8,128)(2,1)S(1)}, s32[1,1]{1,0:T(1,128)}, bf16[64,8,128]{2,1,0:T(8,128)(2,1)S(1)})) conditional(s32[]{:T(128)} %convert_element_type.3, (bf16[16,72,128]{2,1,0:T(8,128)(2,1)S(1)}, f32[16,8]{0,1:T(8,128)}, f32[16,8]{0,1:T(8,128)}) %tuple.11, (s32[1,384]{1,0:T(1,128)}, s32[1,384]{1,0:T(1,128)}, ...), branch_computations={%region_1.0_spmd, %region_2.0_spmd} | conditional | bytes 2758752 | solution.py:273
  29.8 0.8 %copy.11.kern_v_ref = f32[16,8]{1,0:T(8,128)S(1)} copy(f32[16,8]{0,1:T(8,128)} %get-tuple-element.43) | data formatting | bytes 1024 | tf_op jit(solution)/shard_map
  30.5 0.8 %copy.10.kern_u_ref = f32[16,8]{1,0:T(8,128)S(1)} copy(f32[16,8]{0,1:T(8,128)} %get-tuple-element.42) | data formatting | bytes 1024 | tf_op jit(solution)/shard_map
  31.3 3.1 %branch_0_fun.1 = (bf16[72,4096]{1,0:T(8,128)(2,1)S(1)}, s32[1,1]{1,0:T(1,128)}, bf16[64,8,128]{2,1,0:T(8,128)(2,1)S(1)}) custom-call(bf16[16,72,128]{2,1,0:T(8,128)(2,1)S(1)} %get-tuple-element.25.msgs_ref, f32[16,8]{1,0:T(8,128)S(1)} %copy.10.kern_u_ref, f32[16,8]{1,0:T(8,128)S(1)} %copy.11.kern_v_ref), custom_call_target="tpu_custom_call" | custom-call | tf_op jit(solution)/shard_map/cond/branch_0_fun/pallas_call | solution.py:169
  34.4 5.3 %collective-permute-start = (bf16[64,8,128]{2,1,0:T(8,128)(2,1)S(1)}, bf16[64,8,128]{2,1,0:T(8,128)(2,1)S(1)}, u32[]{:S(2)}, u32[]{:S(2)}) collective-permute-start(bf16[64,8,128]{2,1,0:T(8,128)(2,1)S(1)} %get-tuple-element.40), channel_id=1, source_target_pairs={{0,32},{32,64},{64,96},{96,128},{128,160},{160,192},{192,224},{1,3... | collective-permute-start | bytes 393224 | tf_op jit(solution)/shard_map/ppermute | solution.py:274
  39.7 0.8 %copy.15.kern_u_ref = f32[16,8]{1,0:T(8,128)S(1)} copy(f32[16,8]{0,1:T(8,128)} %param.14) | data formatting | bytes 1024 | tf_op args[5]
  40.5 0.8 %copy.16.kern_v_ref = f32[16,8]{1,0:T(8,128)S(1)} copy(f32[16,8]{0,1:T(8,128)} %param.15) | data formatting | bytes 1024 | tf_op args[6]
  41.3 5.5 %shard_map.74.grid_ref = f32[64,64,128]{2,1,0:T(8,128)} custom-call(s32[1,1]{1,0:T(1,128)} %get-tuple-element.38.tiles_ref, bf16[72,4096]{1,0:T(8,128)(2,1)S(1)} %get-tuple-element.39.held_ref, f32[16,8]{1,0:T(8,128)S(1)} %copy.15.kern_u_ref, f32[16,8]{1,0:T(8,128)S(1)} %copy.16.kern_v_ref), custom_call_target="tpu_custom_call" | custom-call | tf_op jit(solution)/shard_map/pallas_call | solution.py:221
  46.8 0.0 collective-permute-done.halo_ref
  46.8 0.0 copy-start
  46.8 0.6 %copy-done = bf16[64,8,128]{2,1,0:T(8,128)(2,1)} copy-done((bf16[64,8,128]{2,1,0:T(8,128)(2,1)}, bf16[64,8,128]{2,1,0:T(8,128)(2,1)S(1)}, u32[]{:S(2)}) %copy-start) | copy-done | bytes 131096
  47.4 1.7 %shard_map.75 = f32[64,64,128]{2,1,0:T(8,128)} custom-call(f32[64,64,128]{2,1,0:T(8,128)} %shard_map.74.grid_ref, bf16[64,8,128]{2,1,0:T(8,128)(2,1)} %copy-done), custom_call_target="tpu_custom_call", output_to_operand_aliasing={{}: (0, {})} | custom-call | tf_op jit(solution)/shard_map/pallas_call | solution.py:245
Async XLA Ops:
  3.9 24.5 %all-to-all-start.1 = ((bf16[16,72,128]{2,1,0:T(8,128)(2,1)}), bf16[16,72,128]{2,1,0:T(8,128)(2,1)S(1)}, u32[]{:S(2)}, u32[]{:S(2)}) async-start(bf16[16,72,128]{2,1,0:T(8,128)(2,1)} %shard_map.73), calls=%async_computation.1 | async-start | bytes 589824 | tf_op jit(solution)/shard_map/all_to_all | solution.py:265
  34.4 12.4 %collective-permute-start = (bf16[64,8,128]{2,1,0:T(8,128)(2,1)S(1)}, bf16[64,8,128]{2,1,0:T(8,128)(2,1)S(1)}, u32[]{:S(2)}, u32[]{:S(2)}) collective-permute-start(bf16[64,8,128]{2,1,0:T(8,128)(2,1)S(1)} %get-tuple-element.40), channel_id=1, source_target_pairs={{0,32},{32,64},{64,96},{96,128},{128,160},{160,192},{192,224},{1,3... | collective-permute-start | bytes 393224 | tf_op jit(solution)/shard_map/ppermute | solution.py:274
  46.8 0.6 %copy-start = (bf16[64,8,128]{2,1,0:T(8,128)(2,1)}, bf16[64,8,128]{2,1,0:T(8,128)(2,1)S(1)}, u32[]{:S(2)}) copy-start(bf16[64,8,128]{2,1,0:T(8,128)(2,1)S(1)} %collective-permute-done.halo_ref) | copy-start | bytes 393220

commit v2 on v1

v2 whole, which is shorter than its diff:
```python
import functools

import jax
import jax.numpy as jnp
from jax import lax
from jax.experimental import pallas as pl
from jax.experimental.pallas import tpu as pltpu
from jax.sharding import PartitionSpec as P

GU = 64
GV = 128
TAPS = 8
LANES = 128
META = 8
KT = 256
F32 = jnp.float32
BF16 = jnp.bfloat16
NT = (((1,), (1,)), ((), ()))


def meta_rows(cap):
    return META * ((cap + LANES - 1) // LANES)


def pack_kernel(cap, n_dst, u_ref, v_ref, w_ref, counts_ref, vis_ref, out_ref):
    chans, rows = vis_ref.shape
    n_blocks = counts_ref.shape[1]
    block = rows // n_blocks
    half = cap // 2
    u, v, w = u_ref[...], v_ref[...], w_ref[...]
    lane = lax.broadcasted_iota(jnp.int32, (1, rows), 1)
    limit = jnp.zeros((1, rows), jnp.int32)
    for b in range(n_blocks):
        limit = jnp.where(lane >= b * block, b * block + counts_ref[0, b], limit)
    live = lane < limit
    first = v // GV
    last = (v + (TAPS - 1)) // GV
    dst = lax.broadcasted_iota(jnp.int32, (n_dst, rows), 0)
    member = ((dst == first) | (dst == last)) & live
    member_f = member.astype(F32)
    before = lax.broadcasted_iota(jnp.int32, (rows, rows), 0) < lax.broadcasted_iota(
        jnp.int32, (rows, rows), 1
    )
    rank = jnp.dot(
        member_f.astype(BF16),
        before.astype(F32).astype(BF16),
        preferred_element_type=F32,
    )
    rank = jnp.where(member, rank.astype(jnp.int32), -1)
    total = jnp.sum(member_f, axis=1, keepdims=True)
    over = (jnp.max(total, axis=0, keepdims=True) > cap).astype(F32)
    meta = jnp.concatenate(
        [
            (u % GU).astype(F32),
            (v % GV).astype(F32),
            first.astype(F32),
            w.astype(F32),
            jnp.zeros((META - 4, rows), F32),
        ],
        axis=0,
    ).astype(BF16)
    vis = vis_ref[...]
    blank = jnp.zeros_like(vis)
    low_lanes = jnp.concatenate([vis, blank], axis=0)
    high_lanes = jnp.concatenate([blank, vis], axis=0)
    slot = lax.broadcasted_iota(jnp.int32, (cap, rows), 0)
    row_id = lax.broadcasted_iota(jnp.int32, (META, 1), 0)
    for d in range(n_dst):
        pick = (slot == rank[d : d + 1, :]).astype(F32).astype(BF16)
        sent = lax.dot_general(pick[:half], low_lanes, NT, preferred_element_type=F32)
        sent += lax.dot_general(pick[half:], high_lanes, NT, preferred_element_type=F32)
        out_ref[d, :half, :] = sent.astype(BF16)
        held = jnp.minimum(total[d : d + 1, :], float(cap))
        coarse = jnp.floor(held / 64.0)
        tail = jnp.where(row_id == 4, over, 0.0)
        tail = jnp.where(row_id == 5, coarse, tail)
        tail = jnp.where(row_id == 6, held - 64.0 * coarse, tail)
        for p in range(0, cap, LANES):
            wide = min(LANES, cap - p)
            tags = lax.dot_general(meta, pick[p : p + wide], NT, preferred_element_type=F32)
            at = half + META * (p // LANES)
            if wide < LANES:
                tags = jnp.concatenate([tags, jnp.zeros((META, LANES - wide), F32)], axis=1)
            out_ref[d, at : at + META, :] = (tags + tail).astype(BF16)


def pack(cap, n_dst, u, v, w, counts, vis):
    vmem = pl.BlockSpec(memory_space=pltpu.VMEM)
    return pl.pallas_call(
        functools.partial(pack_kernel, cap, n_dst),
        out_shape=jax.ShapeDtypeStruct((n_dst, cap // 2 + meta_rows(cap), LANES), BF16),
        in_specs=[vmem, vmem, vmem, pl.BlockSpec(memory_space=pltpu.SMEM), vmem],
        out_specs=vmem,
        compiler_params=pltpu.CompilerParams(vmem_limit_bytes=10 << 20),
    )(u, v, w, counts, vis)


def tap_rows(table, plane):
    result = jnp.zeros((TAPS, plane.shape[1]), F32)
    for p in range(table.shape[1]):
        result = jnp.where(plane == p, table[:, p : p + 1], result)
    return result


def spread(taps, start, low, span):
    cell = lax.broadcasted_iota(jnp.int32, (span, taps.shape[1]), 0) + (low - start)
    result = jnp.zeros((span, taps.shape[1]), F32)
    for t in range(TAPS):
        result = jnp.where(cell == t, taps[t : t + 1, :], result)
    return result


def v_weights(tags, plane, kern_v, facet):
    start = tags[1:2, :] + GV * (tags[2:3, :] - facet)
    wide = spread(tap_rows(kern_v, plane), start, 0, GV)
    high = wide.astype(BF16)
    low = (wide - high.astype(F32)).astype(BF16)
    return jnp.concatenate([high, low], axis=0)


def weighted(vis, ku):
    chans, span, lanes = vis.shape[0], ku.shape[0], vis.shape[1]
    full = vis[:, None, :] * ku[None, :, :]
    return full.reshape(chans * span, lanes).astype(BF16)


def border_kernel(cap, chans, msgs_ref, kern_u_ref, kern_v_ref, held_ref, tiles_ref, halo_ref, rows_s, tags_s, acc):
    n_src = msgs_ref.shape[0]
    half = cap // 2
    facet = lax.axis_index("fv")
    lane = lax.broadcasted_iota(jnp.int32, (META, LANES), 1)

    def put(tile, value):
        tags_s[:, pl.ds(pl.multiple_of(tile * LANES, LANES), LANES)] = value

    lengths = []
    for src in range(n_src):
        tags = msgs_ref[src, half : half + META, :].astype(F32)
        lengths.append((64.0 * tags[5, 0] + tags[6, 0]).astype(jnp.int32))
    offset = 0
    tile = jnp.zeros((META, LANES), F32)
    for src in range(n_src):
        length = lengths[src]
        rows_s[pl.ds(offset, half), :] = msgs_ref[src, :half, :].astype(F32)

        @pl.when(length > half)
        def _(src=src, offset=offset):
            block = msgs_ref[src, :half, :].astype(F32)
            rows_s[pl.ds(offset + half, half), :] = pltpu.roll(block, LANES // 2, 1)

        for p in range(0, cap, LANES):
            at = half + META * (p // LANES)
            tags = msgs_ref[src, at : at + META, :].astype(F32)
            shift = offset % LANES
            turned = pltpu.roll(tags, shift, 1)
            where = offset // LANES
            tile = jnp.where(lane < shift, tile, turned)
            put(where, tile)
            spill = jnp.where(lane < shift, turned, 0.0)
            put(where + 1, spill)
            here = jnp.clip(length - p, 0, LANES)
            tile = jnp.where(shift + here >= LANES, spill, tile)
            offset = offset + here
    rows_s[pl.ds(offset, KT), :] = jnp.zeros((KT, LANES), F32)
    put(offset // LANES + 1, jnp.zeros((META, LANES), F32))
    tiles = jnp.maximum((offset + KT - 1) // KT, 1)
    tiles_ref[0, 0] = tiles
    acc[...] = jnp.zeros_like(acc)
    kern_u, kern_v = kern_u_ref[...], kern_v_ref[...]

    def step(k, _):
        at = pl.multiple_of(k * KT, KT)
        cols = pl.ds(at, KT)
        vis = rows_s[cols, :].T[:chans]
        tags = tags_s[:, cols]
        held_ref[:chans, cols] = vis.astype(BF16)
        held_ref[chans:, cols] = tags.astype(BF16)
        tags = tags.astype(jnp.int32)
        plane = tags[3:4, :]
        ku = spread(tap_rows(kern_u, plane), tags[0:1, :], GU, TAPS)
        left = weighted(vis, ku.astype(BF16).astype(F32))
        right = v_weights(tags, plane, kern_v, facet)
        acc[...] += lax.dot_general(left, right, NT, preferred_element_type=F32)
        return 0

    lax.fori_loop(0, tiles, step, 0)
    halo_ref[...] = (acc[:, :GV] + acc[:, GV:]).reshape(chans, TAPS, GV).astype(BF16)


def border(cap, chans, msgs, kern_u, kern_v, width):
    vmem = pl.BlockSpec(memory_space=pltpu.VMEM)
    return pl.pallas_call(
        functools.partial(border_kernel, cap, chans),
        out_shape=(
            jax.ShapeDtypeStruct((chans + META, width), BF16),
            jax.ShapeDtypeStruct((1, 1), jnp.int32),
            jax.ShapeDtypeStruct((chans, TAPS, GV), BF16),
        ),
        in_specs=[vmem] * 3,
        out_specs=(vmem, pl.BlockSpec(memory_space=pltpu.SMEM), vmem),
        scratch_shapes=[
            pltpu.VMEM((width + 2 * KT, LANES), F32),
            pltpu.VMEM((META, width + 2 * KT), F32),
            pltpu.VMEM((chans * TAPS, 2 * GV), F32),
        ],
        compiler_params=pltpu.CompilerParams(vmem_limit_bytes=12 << 20),
    )(msgs, kern_u, kern_v)


def main_kernel(step_chans, tiles_ref, held_ref, kern_u_ref, kern_v_ref, out_ref, strip_ref, ku_s, kv_s, acc):
    chans = held_ref.shape[0] - META
    facet = lax.axis_index("fv")
    i = pl.program_id(0)
    tiles = tiles_ref[0, 0]

    @pl.when(i == 0)
    def _():
        kern_u, kern_v = kern_u_ref[...], kern_v_ref[...]

        def prepare(k, _):
            cols = pl.ds(pl.multiple_of(k * KT, KT), KT)
            tags = held_ref[chans:, cols].astype(F32).astype(jnp.int32)
            plane = tags[3:4, :]
            ku_s[:, cols] = spread(tap_rows(kern_u, plane), tags[0:1, :], 0, GU).astype(BF16)
            start = tags[1:2, :] + GV * (tags[2:3, :] - facet)
            wide = spread(tap_rows(kern_v, plane), start, 0, GV).T
            high = wide.astype(BF16)
            kv_s[cols, :GV] = high
            kv_s[cols, GV:] = (wide - high.astype(F32)).astype(BF16)
            return 0

        lax.fori_loop(0, tiles, prepare, 0)

    first = pl.multiple_of(i * step_chans, step_chans)

    def emit(total):
        total = (total[:, :GV] + total[:, GV:]).reshape(step_chans, GU, GV)
        out_ref[...] = total
        strip_ref[pl.ds(first, step_chans)] = total[:, :TAPS, :]

    def product(cols):
        vis = held_ref[pl.ds(first, step_chans), cols].astype(F32)
        left = weighted(vis, ku_s[:, cols].astype(F32))
        return jnp.dot(left, kv_s[cols, :], preferred_element_type=F32)

    for n in (1, 2, 3):

        @pl.when(tiles == n)
        def _(n=n):
            emit(product(pl.ds(0, n * KT)))

    @pl.when(tiles > 3)
    def _():
        acc[...] = jnp.zeros_like(acc)

        def step(k, _):
            acc[...] += product(pl.ds(pl.multiple_of(k * KT, KT), KT))
            return 0

        lax.fori_loop(0, tiles, step, 0)
        emit(acc[...])


def main(tiles, held, kern_u, kern_v, step_chans=16):
    depth, width = held.shape
    chans = depth - META
    vmem = pl.BlockSpec(memory_space=pltpu.VMEM)
    return pl.pallas_call(
        functools.partial(main_kernel, step_chans),
        grid=(chans // step_chans,),
        out_shape=(
            jax.ShapeDtypeStruct((chans, GU, GV), F32),
            jax.ShapeDtypeStruct((chans, TAPS, GV), F32),
        ),
        in_specs=[pl.BlockSpec(memory_space=pltpu.SMEM)] + [vmem] * 3,
        out_specs=(
            pl.BlockSpec((step_chans, GU, GV), lambda i: (i, 0, 0)),
            vmem,
        ),
        scratch_shapes=[
            pltpu.VMEM((GU, width), BF16),
            pltpu.VMEM((width, 2 * GV), BF16),
            pltpu.VMEM((step_chans * GU, 2 * GV), F32),
        ],
        compiler_params=pltpu.CompilerParams(
            dimension_semantics=("arbitrary",), vmem_limit_bytes=16 << 20
        ),
    )(tiles, held, kern_u, kern_v)


def join_kernel(_, strip_ref, halo_ref, out_ref, total, sem):
    total[...] = strip_ref[...] + halo_ref[...].astype(F32)
    copy = pltpu.make_async_copy(total, out_ref.at[:, pl.ds(0, TAPS), :], sem)
    copy.start()
    copy.wait()


def join(grid, strip, halo):
    vmem = pl.BlockSpec(memory_space=pltpu.VMEM)
    whole = pl.BlockSpec(memory_space=pl.ANY)
    return pl.pallas_call(
        join_kernel,
        out_shape=jax.ShapeDtypeStruct(grid.shape, grid.dtype),
        in_specs=[whole, vmem, vmem],
        out_specs=whole,
        scratch_shapes=[pltpu.VMEM(strip.shape, F32), pltpu.SemaphoreType.DMA(())],
        input_output_aliases={0: 0},
        compiler_params=pltpu.CompilerParams(vmem_limit_bytes=2 << 20),
    )(grid, strip, halo)


def per_device(u_cell, v_cell, w_plane, counts, vis_values, kern_u, kern_v):
    n_fv = lax.axis_size("fv")
    n_fu = lax.axis_size("fu")
    rows = u_cell.shape[1]
    chans = vis_values.shape[0]
    width = 4096
    small = 80
    vis = vis_values[:, 0, :]
    kern_u, kern_v = kern_u.T, kern_v.T

    def exchange(cap):
        sent = pack(cap, n_fv, u_cell, v_cell, w_plane, counts, vis)
        return lax.all_to_all(sent, "fv", 0, 0)

    msgs = exchange(small)
    over = jnp.max(msgs[:, small // 2 + 4, 0]) > 0

    def whole():
        return border(rows, chans, exchange(rows), kern_u, kern_v, width)

    def usual():
        return border(small, chans, msgs, kern_u, kern_v, width)

    held, tiles, halo = lax.cond(over, whole, usual)
    came = lax.ppermute(halo, "fu", [(i, i + 1) for i in range(n_fu - 1)])
    grid, strip = main(tiles, held, kern_u, kern_v)
    return join(grid, strip, came)


def solution(mesh):
    return jax.shard_map(
        per_device,
        mesh=mesh,
        in_specs=(
            P("fu", "fv"),
            P("fu", "fv"),
            P("fu", "fv"),
            P("fu", "fv"),
            P("ch", "fu", "fv"),
            P(),
            P(),
        ),
        out_specs=P("ch", "fu", "fv"),
        check_vma=False,
    )
```

time: 49.6 us -> 40.1 us (0.81)
  local copies, waits for them, and re-layouts: 4.55 us -> 0 us
  Pallas kernels: 13.4 us -> 10.3 us
  waiting for transfers between devices: 12.8 us -> 10.8 us
    unnamed x5 -> x0, local copies, waits for them, and re-layouts: 3.04 us -> none
    all_to_all x1, waiting for transfers between devices: 12.8 us -> 10.8 us  [exchange(): return lax.all_to_all(sent, 'fv', 0, 0)]
    pallas_call x2, Pallas kernels: 4.82 us -> 3.13 us  [the longest x1 2.39 us: border(): pl.pallas_call(functools.partial(border_kernel, cap, chans), out_shape=(j...]
    another operation x2 -> x0, local copies, waits for them, and re-layouts: 1.52 us -> none
    pallas_call x1, Pallas kernels: 5.51 us -> 4.13 us  [main(): pl.pallas_call(functools.partial(main_kernel, step_chans), grid=(chans //...]
  transfers between devices with their start and end apart: 2 -> 2, of which waited for: 1 -> 1; matrix products, arithmetic and copies ran while one was open for 3% -> 0% of each run, Pallas kernels for 11% -> 10%
where the time goes in v2:
time: 40.1 us; the launch traced here: 39.7 us
  starting transfers between devices  17.3 us (43%)
  waiting for transfers between devices  10.8 us (27%)
  Pallas kernels  10.3 us (26%)
  between operations  0.68 us (2%)
  other arithmetic  0.62 us (2%)
    all_to_all x1, starting transfers between devices, exchange(): return lax.all_to_all(sent, 'fv', 0, 0)  11.7 us
    all_to_all x1, waiting for transfers between devices, exchange(): return lax.all_to_all(sent, 'fv', 0, 0)  10.8 us
    ppermute x1, starting transfers between devices, per_device(): came = lax.ppermute(halo, 'fu', [(i, i + 1) for i in range(n_fu - 1)])  5.57 us
    pallas_call x1, Pallas kernels, main(): pl.pallas_call(functools.partial(main_kernel, step_chans), grid=(chans //...  4.13 us
    pallas_call x1, Pallas kernels, pack(): pl.pallas_call(functools.partial(pack_kernel, cap, n_dst), out_shape=jax....  2.99 us
    pallas_call x1, Pallas kernels, border(): pl.pallas_call(functools.partial(border_kernel, cap, chans), out_shape=(j...  2.39 us
  transfers between devices with their start and end apart: 2, of which 1 were waited for; matrix products, arithmetic and copies ran while one was open for 0% of the time, Pallas kernels for 10%

profile of v2, /device:TPU:1, one launch (start us, length us, event | category | flops | bytes accessed | tf_op | source)
XLA Modules:
  0.0 39.7 jit_solution(8755031103365698660)
XLA Ops:
  0.0 3.0 %shard_map.73 = bf16[16,48,128]{2,1,0:T(8,128)(2,1)} custom-call(s32[1,384]{1,0:T(1,128)} %u_ref.1, s32[1,384]{1,0:T(1,128)} %v_ref.1, s32[1,384]{1,0:T(1,128)} %w_ref.1, s32[1,3]{1,0:T(1,128)} %counts_ref.1, bf16[64,384]{1,0:T(8,128)(2,1)} %bitcast.3), custom_call_target="tpu_custom_call" | custom-call | tf_op jit(solution)/shard_map/pallas_call | solution.py:89
  3.0 11.7 %all-to-all-start.1 = ((bf16[16,48,128]{2,1,0:T(8,128)(2,1)}), bf16[16,48,128]{2,1,0:T(8,128)(2,1)S(1)}, u32[]{:S(2)}, u32[]{:S(2)}) async-start(bf16[16,48,128]{2,1,0:T(8,128)(2,1)} %shard_map.73), calls=%async_computation.1 | async-start | bytes 393216 | tf_op jit(solution)/shard_map/all_to_all | solution.py:324
  14.8 10.8 %all-to-all-done.1 = bf16[16,48,128]{2,1,0:T(8,128)(2,1)S(1)} async-done(((bf16[16,48,128]{2,1,0:T(8,128)(2,1)}), bf16[16,48,128]{2,1,0:T(8,128)(2,1)S(1)}, u32[]{:S(2)}, u32[]{:S(2)}) %all-to-all-start.1) | async-done | bytes 196640 | tf_op jit(solution)/shard_map/all_to_all | solution.py:324
  25.5 0.6 %slice_reduce_fusion = bf16[]{:T(256)} fusion(bf16[16,48,128]{2,1,0:T(8,128)(2,1)S(1)} %all-to-all-done.1), kind=kLoop, calls=%fused_computation | loop fusion | flops 15 | bytes 34 | tf_op jit(solution)/shard_map/reduce_max | solution.py:327
  26.8 2.4 %conditional.1 = ((bf16[72,4096]{1,0:T(8,128)(2,1)S(1)}, s32[1,1]{1,0:T(1,128)}, bf16[64,8,128]{2,1,0:T(8,128)(2,1)S(1)})) conditional(s32[]{:T(128)} %convert_element_type.3, (bf16[16,48,128]{2,1,0:T(8,128)(2,1)S(1)}, f32[8,16]{1,0:T(8,128)}, f32[8,16]{1,0:T(8,128)}) %tuple.20, (s32[1,384]{1,0:T(1,128)}, s32[1,384]{1,0:T(1,128)}, ...), branch_computations={%region_1.0_spmd, %region_2.0_spmd} | conditional | bytes 1773632 | solution.py:335
  26.8 2.4 %branch_0_fun.1 = (bf16[72,4096]{1,0:T(8,128)(2,1)S(1)}, s32[1,1]{1,0:T(1,128)}, bf16[64,8,128]{2,1,0:T(8,128)(2,1)S(1)}) custom-call(bf16[16,48,128]{2,1,0:T(8,128)(2,1)S(1)} %get-tuple-element.25.msgs_ref, f32[8,16]{1,0:T(8,128)} %get-tuple-element.26.kern_u_ref, f32[8,16]{1,0:T(8,128)} %get-tuple-element.27.kern_v_ref), custom_call_target="tpu_custom_call" | custom-call | tf_op jit(solution)/shard_map/cond/branch_0_fun/pallas_call | solution.py:192
  29.2 5.6 %collective-permute-start = (bf16[64,8,128]{2,1,0:T(8,128)(2,1)S(1)}, bf16[64,8,128]{2,1,0:T(8,128)(2,1)S(1)}, u32[]{:S(2)}, u32[]{:S(2)}) collective-permute-start(bf16[64,8,128]{2,1,0:T(8,128)(2,1)S(1)} %get-tuple-element.44), channel_id=1, source_target_pairs={{0,32},{32,64},{64,96},{96,128},{128,160},{160,192},{192,224},{1,3... | collective-permute-start | bytes 393224 | tf_op jit(solution)/shard_map/ppermute | solution.py:336
  34.8 4.1 %shard_map.74 = (f32[64,64,128]{2,1,0:T(8,128)}, f32[64,8,128]{2,1,0:T(8,128)S(1)}) custom-call(s32[1,1]{1,0:T(1,128)} %get-tuple-element.40.tiles_ref, bf16[72,4096]{1,0:T(8,128)(2,1)S(1)} %get-tuple-element.41.held_ref, f32[8,16]{1,0:T(8,128)} %bitcast.7, f32[8,16]{1,0:T(8,128)} %bitcast.10), custom_call_target="tpu_custom_call" | custom-call | tf_op jit(solution)/shard_map/pallas_call | solution.py:268
  38.9 0.0 collective-permute-done.halo_ref
  38.9 0.7 %shard_map.75 = f32[64,64,128]{2,1,0:T(8,128)} custom-call(f32[64,64,128]{2,1,0:T(8,128)} %get-tuple-element.42._, f32[64,8,128]{2,1,0:T(8,128)S(1)} %get-tuple-element.43.strip_ref, bf16[64,8,128]{2,1,0:T(8,128)(2,1)S(1)} %collective-permute-done.halo_ref), custom_call_target="tpu_custom_call", output_to_operand_aliasing={{}: (0, {})} | custom-call | tf_op jit(solution)/shard_map/pallas_call | solution.py:301
Async XLA Ops:
  3.0 22.5 %all-to-all-start.1 = ((bf16[16,48,128]{2,1,0:T(8,128)(2,1)}), bf16[16,48,128]{2,1,0:T(8,128)(2,1)S(1)}, u32[]{:S(2)}, u32[]{:S(2)}) async-start(bf16[16,48,128]{2,1,0:T(8,128)(2,1)} %shard_map.73), calls=%async_computation.1 | async-start | bytes 393216 | tf_op jit(solution)/shard_map/all_to_all | solution.py:324
  29.2 9.7 %collective-permute-start = (bf16[64,8,128]{2,1,0:T(8,128)(2,1)S(1)}, bf16[64,8,128]{2,1,0:T(8,128)(2,1)S(1)}, u32[]{:S(2)}, u32[]{:S(2)}) collective-permute-start(bf16[64,8,128]{2,1,0:T(8,128)(2,1)S(1)} %get-tuple-element.44), channel_id=1, source_target_pairs={{0,32},{32,64},{64,96},{96,128},{128,160},{160,192},{192,224},{1,3... | collective-permute-start | bytes 393224 | tf_op jit(solution)/shard_map/ppermute | solution.py:336

commit v3 on v2

v3 whole, which is shorter than its diff:
```python
import functools

import jax
import jax.numpy as jnp
from jax import lax
from jax.experimental import pallas as pl
from jax.experimental.pallas import tpu as pltpu
from jax.sharding import PartitionSpec as P

GU = 64
GV = 128
TAPS = 8
LANES = 128
META = 8
KT = 256
F32 = jnp.float32
BF16 = jnp.bfloat16
NT = (((1,), (1,)), ((), ()))


def tag_rows(half):
    per_row = LANES // (2 * META)
    return META * (-(-half // (META * per_row)))


def pack_kernel(
    half, n_dst, u_ref, v_ref, w_ref, counts_ref, vis_ref, kern_u_ref, kern_v_ref, out_ref, tables_ref, picks_s
):
    chans, rows = vis_ref.shape
    n_blocks = counts_ref.shape[1]
    block = rows // n_blocks
    cap = 2 * half
    tables_ref[:TAPS, :] = kern_u_ref[...]
    tables_ref[TAPS:, :] = kern_v_ref[...]
    u, v, w = u_ref[...], v_ref[...], w_ref[...]
    lane = lax.broadcasted_iota(jnp.int32, (1, rows), 1)
    limit = jnp.zeros((1, rows), jnp.int32)
    for b in range(n_blocks):
        limit = jnp.where(lane >= b * block, b * block + counts_ref[0, b], limit)
    live = lane < limit
    first = v // GV
    last = (v + (TAPS - 1)) // GV
    dst = lax.broadcasted_iota(jnp.int32, (n_dst, rows), 0)
    member = ((dst == first) | (dst == last)) & live
    member_f = member.astype(F32)
    before = lax.broadcasted_iota(jnp.int32, (rows, rows), 0) < lax.broadcasted_iota(
        jnp.int32, (rows, rows), 1
    )
    rank = jnp.dot(
        member_f.astype(BF16),
        before.astype(F32).astype(BF16),
        preferred_element_type=F32,
    )
    rank = jnp.where(member, rank.astype(jnp.int32), -1)
    total = jnp.sum(member_f, axis=1, keepdims=True)
    over = (jnp.max(total, axis=0, keepdims=True) > cap).astype(F32)
    tags = jnp.concatenate(
        [
            (u % GU).astype(F32),
            (v % GV).astype(F32),
            first.astype(F32),
            w.astype(F32),
            jnp.zeros((META - 4, rows), F32),
        ],
        axis=0,
    )
    empty = jnp.zeros_like(tags)
    tags = jnp.concatenate(
        [
            jnp.concatenate([tags, empty], axis=1),
            jnp.concatenate([empty, tags], axis=1),
            jnp.zeros((LANES - 2 * META, 2 * rows), F32),
        ],
        axis=0,
    ).astype(BF16)
    vis = vis_ref[...]
    blank = jnp.zeros_like(vis)
    source = jnp.concatenate(
        [
            jnp.concatenate([vis, blank], axis=1),
            jnp.concatenate([blank, vis], axis=1),
            tags,
        ],
        axis=0,
    )
    slot = lax.broadcasted_iota(jnp.int32, (cap, rows), 0)
    for d in range(n_dst):
        pick = (slot == rank[d : d + 1, :]).astype(F32).astype(BF16)
        picks_s[d * half : (d + 1) * half, :rows] = pick[:half]
        picks_s[d * half : (d + 1) * half, rows:] = pick[half:]
    sent = lax.dot_general(picks_s[...], source, NT, preferred_element_type=F32)
    out_ref[:, :half, :] = sent[:, :LANES].reshape(n_dst, half, LANES).astype(BF16)
    place = lax.broadcasted_iota(jnp.int32, (META, LANES), 1)
    per_row = LANES // (2 * META)
    for d in range(n_dst):
        held = jnp.minimum(total[d : d + 1, :], float(cap))
        coarse = jnp.floor(held / 64.0)
        row = jnp.where(place == 4, over, 0.0)
        row = jnp.where(place == 5, coarse, row)
        row = jnp.where(place == 6, held - 64.0 * coarse, row)
        for g in range(half // META):
            at = d * half + g * META
            part = sent[at : at + META, LANES:]
            shift = 2 * META * (g % per_row)
            row = row + (pltpu.roll(part, shift, 1) if shift else part)
            if g % per_row == per_row - 1 or g == half // META - 1:
                to = half + META * (g // per_row)
                out_ref[d, to : to + META, :] = row.astype(BF16)
                row = jnp.zeros((META, LANES), F32)


def pack(half, n_dst, u, v, w, counts, vis, kern_u, kern_v):
    vmem = pl.BlockSpec(memory_space=pltpu.VMEM)
    rows = u.shape[1]
    return pl.pallas_call(
        functools.partial(pack_kernel, half, n_dst),
        out_shape=(
            jax.ShapeDtypeStruct((n_dst, half + tag_rows(half), LANES), BF16),
            jax.ShapeDtypeStruct((2 * TAPS, kern_u.shape[1]), F32),
        ),
        in_specs=[vmem, vmem, vmem, pl.BlockSpec(memory_space=pltpu.SMEM), vmem, vmem, vmem],
        out_specs=(vmem, vmem),
        scratch_shapes=[pltpu.VMEM((n_dst * half, 2 * rows), BF16)],
        compiler_params=pltpu.CompilerParams(vmem_limit_bytes=(8 << 20) if half <= 64 else (24 << 20)),
    )(u, v, w, counts, vis, kern_u, kern_v)


def tap_rows(table, plane):
    result = jnp.zeros((TAPS, plane.shape[1]), F32)
    for p in range(table.shape[1]):
        result = jnp.where(plane == p, table[:, p : p + 1], result)
    return result


def spread(taps, start, low, span):
    cell = lax.broadcasted_iota(jnp.int32, (span, taps.shape[1]), 0) + (low - start)
    result = jnp.zeros((span, taps.shape[1]), F32)
    for t in range(TAPS):
        result = jnp.where(cell == t, taps[t : t + 1, :], result)
    return result


def v_weights(tags, plane, kern_v, facet):
    start = tags[1:2, :] + GV * (tags[2:3, :] - facet)
    wide = spread(tap_rows(kern_v, plane), start, 0, GV)
    high = wide.astype(BF16)
    low = (wide - high.astype(F32)).astype(BF16)
    return jnp.concatenate([high, low], axis=0)


def weighted(vis, ku):
    chans, span, lanes = vis.shape[0], ku.shape[0], vis.shape[1]
    full = vis[:, None, :] * ku[None, :, :]
    return full.reshape(chans * span, lanes).astype(BF16)


def border_kernel(half, chans, msgs_ref, tables_ref, held_ref, halo_ref, rows_s, acc):
    n_src = msgs_ref.shape[0]
    facet = lax.axis_index("fv")
    lane = lax.broadcasted_iota(jnp.int32, (META, LANES), 1)
    per_row = LANES // (2 * META)

    lengths = []
    for src in range(n_src):
        tags = msgs_ref[src, half : half + META, :].astype(F32)
        lengths.append((64.0 * tags[0, 5] + tags[0, 6]).astype(jnp.int32))

    def rows_of(src, upper):
        tags = msgs_ref[src, half:, :].astype(F32)
        vis = msgs_ref[src, :half, :].astype(F32)
        if upper:
            vis = pltpu.roll(vis, LANES // 2, 1)
        parts = []
        for g in range(half // META):
            at = META * (g // per_row)
            shift = (chans - 2 * META * (g % per_row) - META * upper) % LANES
            tag = pltpu.roll(tags[at : at + META], shift, 1)
            parts.append(jnp.where(lane < chans, vis[g * META : (g + 1) * META], tag))
        return jnp.concatenate(parts, axis=0)

    offset = 0
    for src in range(n_src):
        rows_s[pl.ds(offset, half), :] = rows_of(src, 0)

        @pl.when(lengths[src] > half)
        def _(src=src, offset=offset):
            rows_s[pl.ds(offset + half, half), :] = rows_of(src, 1)

        offset = offset + lengths[src]
    rows_s[pl.ds(offset, KT), :] = jnp.zeros((KT, LANES), F32)
    tiles = jnp.maximum((offset + KT - 1) // KT, 1)
    acc[...] = jnp.zeros_like(acc)
    kern_u, kern_v = tables_ref[:TAPS, :], tables_ref[TAPS:, :]
    tag_id = lax.broadcasted_iota(jnp.int32, (META, KT), 0)

    def step(k, _):
        cols = pl.ds(pl.multiple_of(k * KT, KT), KT)
        turned = rows_s[cols, :].T
        vis, tags = turned[:chans], turned[chans : chans + META]
        held_ref[:chans, cols] = vis.astype(BF16)
        held_ref[chans:, cols] = jnp.where(tag_id == META - 1, tiles.astype(F32), tags).astype(BF16)
        tags = tags.astype(jnp.int32)
        plane = tags[3:4, :]
        ku = spread(tap_rows(kern_u, plane), tags[0:1, :], GU, TAPS)
        left = weighted(vis, ku.astype(BF16).astype(F32))
        right = v_weights(tags, plane, kern_v, facet)
        acc[...] += lax.dot_general(left, right, NT, preferred_element_type=F32)
        return 0

    lax.fori_loop(0, tiles, step, 0)
    halo_ref[...] = (acc[:, :GV] + acc[:, GV:]).reshape(chans, TAPS, GV).astype(BF16)


def border(half, chans, msgs, tables, width):
    vmem = pl.BlockSpec(memory_space=pltpu.VMEM)
    return pl.pallas_call(
        functools.partial(border_kernel, half, chans),
        out_shape=(
            jax.ShapeDtypeStruct((chans + META, width), BF16),
            jax.ShapeDtypeStruct((chans, TAPS, GV), BF16),
        ),
        in_specs=[vmem, vmem],
        out_specs=(vmem, vmem),
        scratch_shapes=[
            pltpu.VMEM((width + 2 * KT, LANES), F32),
            pltpu.VMEM((chans * TAPS, 2 * GV), F32),
        ],
        compiler_params=pltpu.CompilerParams(vmem_limit_bytes=12 << 20),
    )(msgs, tables)


def main_kernel(step_chans, held_ref, tables_ref, out_ref, strip_ref, grid_s, ku_s, kv_s, acc, sems):
    chans = held_ref.shape[0] - META
    facet = lax.axis_index("fv")
    kern_u, kern_v = tables_ref[:TAPS, :], tables_ref[TAPS:, :]
    tiles = held_ref[chans:, :LANES].astype(F32)[META - 1, 0].astype(jnp.int32)

    def prepare(k):
        cols = pl.ds(pl.multiple_of(k * KT, KT), KT)
        tags = held_ref[chans:, cols].astype(F32).astype(jnp.int32)
        plane = tags[3:4, :]
        ku_s[:, cols] = spread(tap_rows(kern_u, plane), tags[0:1, :], 0, GU).astype(BF16)
        start = tags[1:2, :] + GV * (tags[2:3, :] - facet)
        wide = spread(tap_rows(kern_v, plane), start, 0, GV).T
        high = wide.astype(BF16)
        kv_s[cols, :GV] = high
        kv_s[cols, GV:] = (wide - high.astype(F32)).astype(BF16)

    def product(first, cols):
        vis = held_ref[pl.ds(first, step_chans), cols].astype(F32)
        left = weighted(vis, ku_s[:, cols].astype(F32))
        return jnp.dot(left, kv_s[cols, :], preferred_element_type=F32)

    def copy_out(i):
        some = pl.ds(i * step_chans, step_chans)
        return pltpu.make_async_copy(grid_s.at[some], out_ref.at[some], sems.at[i])

    def emit(i, total):
        total = (total[:, :GV] + total[:, GV:]).reshape(step_chans, GU, GV)
        some = pl.ds(i * step_chans, step_chans)
        grid_s[some] = total
        strip_ref[some] = total[:, :TAPS, :]
        copy_out(i).start()

    steps = chans // step_chans
    for n in (1, 2, 3):

        @pl.when(tiles == n)
        def _(n=n):
            for k in range(n):
                prepare(k)
            for i in range(steps):
                emit(i, product(i * step_chans, pl.ds(0, n * KT)))

    @pl.when(tiles > 3)
    def _():
        lax.fori_loop(0, tiles, lambda k, _: (prepare(k), 0)[1], 0)
        for i in range(steps):
            acc[...] = jnp.zeros_like(acc)

            def step(k, _, i=i):
                acc[...] += product(i * step_chans, pl.ds(pl.multiple_of(k * KT, KT), KT))
                return 0

            lax.fori_loop(0, tiles, step, 0)
            emit(i, acc[...])

    for i in range(steps):
        copy_out(i).wait()


def main(held, tables, step_chans=16):
    depth, width = held.shape
    chans = depth - META
    vmem = pl.BlockSpec(memory_space=pltpu.VMEM)
    return pl.pallas_call(
        functools.partial(main_kernel, step_chans),
        out_shape=(
            jax.ShapeDtypeStruct((chans, GU, GV), F32),
            jax.ShapeDtypeStruct((chans, TAPS, GV), F32),
        ),
        in_specs=[vmem, vmem],
        out_specs=(pl.BlockSpec(memory_space=pl.ANY), vmem),
        scratch_shapes=[
            pltpu.VMEM((chans, GU, GV), F32),
            pltpu.VMEM((GU, width), BF16),
            pltpu.VMEM((width, 2 * GV), BF16),
            pltpu.VMEM((step_chans * GU, 2 * GV), F32),
            pltpu.SemaphoreType.DMA((chans // step_chans,)),
        ],
        compiler_params=pltpu.CompilerParams(vmem_limit_bytes=18 << 20),
    )(held, tables)


def join_kernel(_, strip_ref, halo_ref, out_ref, total, sem):
    total[...] = strip_ref[...] + halo_ref[...].astype(F32)
    copy = pltpu.make_async_copy(total, out_ref.at[:, pl.ds(0, TAPS), :], sem)
    copy.start()
    copy.wait()


def join(grid, strip, halo):
    vmem = pl.BlockSpec(memory_space=pltpu.VMEM)
    whole = pl.BlockSpec(memory_space=pl.ANY)
    return pl.pallas_call(
        join_kernel,
        out_shape=jax.ShapeDtypeStruct(grid.shape, grid.dtype),
        in_specs=[whole, vmem, vmem],
        out_specs=whole,
        scratch_shapes=[pltpu.VMEM(strip.shape, F32), pltpu.SemaphoreType.DMA(())],
        input_output_aliases={0: 0},
        compiler_params=pltpu.CompilerParams(vmem_limit_bytes=2 << 20),
    )(grid, strip, halo)


def per_device(u_cell, v_cell, w_plane, counts, vis_values, kern_u, kern_v):
    n_fv = lax.axis_size("fv")
    n_fu = lax.axis_size("fu")
    rows = u_cell.shape[1]
    chans = vis_values.shape[0]
    width = 4096
    usual_half = 40
    vis = vis_values[:, 0, :]

    def exchange(half):
        sent, tables = pack(half, n_fv, u_cell, v_cell, w_plane, counts, vis, kern_u.T, kern_v.T)
        return lax.all_to_all(sent, "fv", 0, 0), tables

    msgs, tables = exchange(usual_half)
    over = jnp.any(msgs[:, usual_half, 4] > 0)

    def whole():
        return border(rows // 2, chans, exchange(rows // 2)[0], tables, width)

    def usual():
        return border(usual_half, chans, msgs, tables, width)

    held, halo = lax.cond(over, whole, usual)
    came = lax.ppermute(halo, "fu", [(i, i + 1) for i in range(n_fu - 1)])
    grid, strip = main(held, tables)
    return join(grid, strip, came)


def solution(mesh):
    return jax.shard_map(
        per_device,
        mesh=mesh,
        in_specs=(
            P("fu", "fv"),
            P("fu", "fv"),
            P("fu", "fv"),
            P("fu", "fv"),
            P("ch", "fu", "fv"),
            P(),
            P(),
        ),
        out_specs=P("ch", "fu", "fv"),
        check_vma=False,
    )
```

time: 40.1 us -> 36.6 us (0.913)
  Pallas kernels: 10.3 us -> 6.78 us
    pallas_call x3, Pallas kernels: 9.52 us -> 6.04 us  [the longest x1 2.16 us: pack(): pl.pallas_call(functools.partial(pack_kernel, half, n_dst), out_shape=(ja...]
    reduce_or x0 -> x1, other arithmetic: none -> 0.72 us  [per_device(): over = jnp.any(msgs[:, usual_half, 4] > 0)]
    reduce_max x1 -> x0, other arithmetic: 0.62 us -> none  [per_device(): over = jnp.max(msgs[:, small // 2 + 4, 0]) > 0]
  transfers between devices with their start and end apart: 2 -> 2, of which waited for: 1 -> 1; matrix products, arithmetic and copies ran while one was open for 0% -> 0% of each run, Pallas kernels for 10% -> 6%
where the time goes in v3:
time: 36.6 us; the launch traced here: 36.3 us
  starting transfers between devices  17.3 us (47%)
  waiting for transfers between devices  10.8 us (30%)
  Pallas kernels  6.78 us (19%)
  other arithmetic  0.72 us (2%)
  between operations  0.69 us (2%)
    all_to_all x1, starting transfers between devices, exchange(): return (lax.all_to_all(sent, 'fv', 0, 0), tables)  11.7 us
    all_to_all x1, waiting for transfers between devices, exchange(): return (lax.all_to_all(sent, 'fv', 0, 0), tables)  10.8 us
    ppermute x1, starting transfers between devices, per_device(): came = lax.ppermute(halo, 'fu', [(i, i + 1) for i in range(n_fu - 1)])  5.58 us
    pallas_call x1, Pallas kernels, pack(): pl.pallas_call(functools.partial(pack_kernel, half, n_dst), out_shape=(ja...  2.16 us
    pallas_call x1, Pallas kernels, main(): pl.pallas_call(functools.partial(main_kernel, step_chans), out_shape=(jax...  2.11 us
    pallas_call x1, Pallas kernels, border(): pl.pallas_call(functools.partial(border_kernel, half, chans), out_shape=(...  1.76 us
    pallas_call x1, Pallas kernels, join(): pl.pallas_call(join_kernel, out_shape=jax.ShapeDtypeStruct(grid.shape, gr...  0.74 us
  transfers between devices with their start and end apart: 2, of which 1 were waited for; matrix products, arithmetic and copies ran while one was open for 0% of the time, Pallas kernels for 6%

profile of v3, /device:TPU:1, one launch (start us, length us, event | category | flops | bytes accessed | tf_op | source)
XLA Modules:
  0.0 36.3 jit_solution(17595898041186107176)
XLA Ops:
  0.0 2.2 %shard_map.73 = (bf16[16,48,128]{2,1,0:T(8,128)(2,1)}, f32[16,16]{1,0:T(8,128)S(1)}) custom-call(s32[1,384]{1,0:T(1,128)} %u_ref.1, s32[1,384]{1,0:T(1,128)} %v_ref.1, s32[1,384]{1,0:T(1,128)} %w_ref.1, s32[1,3]{1,0:T(1,128)} %counts_ref.1, bf16[64,384]{1,0:T(8,128)(2,1)} %bitcast.5, f32[8,16]{1,0:T(8,128)} %bitcast.7, f32[8,16]{1,0:T(8,128)} %bitcast.9), custom_call_target="tpu_custom_call" | custom-call | tf_op jit(solution)/shard_map/pallas_call | solution.py:115
  2.2 11.7 %all-to-all-start.1 = ((bf16[16,48,128]{2,1,0:T(8,128)(2,1)}), bf16[16,48,128]{2,1,0:T(8,128)(2,1)S(1)}, u32[]{:S(2)}, u32[]{:S(2)}) async-start(bf16[16,48,128]{2,1,0:T(8,128)(2,1)} %get-tuple-element.42), calls=%async_computation.1 | async-start | bytes 393216 | tf_op jit(solution)/shard_map/all_to_all | solution.py:347
  13.9 10.8 %all-to-all-done.1 = bf16[16,48,128]{2,1,0:T(8,128)(2,1)S(1)} async-done(((bf16[16,48,128]{2,1,0:T(8,128)(2,1)}), bf16[16,48,128]{2,1,0:T(8,128)(2,1)S(1)}, u32[]{:S(2)}, u32[]{:S(2)}) %all-to-all-start.1) | async-done | bytes 196640 | tf_op jit(solution)/shard_map/all_to_all | solution.py:347
  24.7 0.7 %compare_reduce_fusion = pred[]{:T(512)} fusion(bf16[16,48,128]{2,1,0:T(8,128)(2,1)S(1)} %all-to-all-done.1), kind=kLoop, calls=%fused_computation | loop fusion | flops 31 | bytes 33 | tf_op jit(solution)/shard_map/reduce_or | solution.py:350
  26.1 1.8 %conditional.1 = ((bf16[72,4096]{1,0:T(8,128)(2,1)S(1)}, bf16[64,8,128]{2,1,0:T(8,128)(2,1)S(1)})) conditional(s32[]{:T(128)} %convert_element_type.3, (bf16[16,48,128]{2,1,0:T(8,128)(2,1)S(1)}, f32[16,16]{1,0:T(8,128)S(1)}) %tuple.11, (f32[16,8]{0,1:T(8,128)}, f32[16,8]{0,1:T(8,128)}, s32[1,384]{1,0:T(1,128)}, s32[1,384]{1,0:T(1,128)}, ...), branch_computations={%region_1.0_spmd, %region_2.0_spmd} | conditional | bytes 1769480 | solution.py:358
  26.1 1.8 %branch_0_fun.1 = (bf16[72,4096]{1,0:T(8,128)(2,1)S(1)}, bf16[64,8,128]{2,1,0:T(8,128)(2,1)S(1)}) custom-call(bf16[16,48,128]{2,1,0:T(8,128)(2,1)S(1)} %get-tuple-element.25.msgs_ref, f32[16,16]{1,0:T(8,128)S(1)} %get-tuple-element.26.tables_ref), custom_call_target="tpu_custom_call" | custom-call | tf_op jit(solution)/shard_map/cond/branch_0_fun/pallas_call | solution.py:216
  27.8 5.6 %collective-permute-start = (bf16[64,8,128]{2,1,0:T(8,128)(2,1)S(1)}, bf16[64,8,128]{2,1,0:T(8,128)(2,1)S(1)}, u32[]{:S(2)}, u32[]{:S(2)}) collective-permute-start(bf16[64,8,128]{2,1,0:T(8,128)(2,1)S(1)} %get-tuple-element.47), channel_id=1, source_target_pairs={{0,32},{32,64},{64,96},{96,128},{128,160},{160,192},{192,224},{1,3... | collective-permute-start | bytes 393224 | tf_op jit(solution)/shard_map/ppermute | solution.py:359
  33.4 2.1 %shard_map.74 = (f32[64,64,128]{2,1,0:T(8,128)}, f32[64,8,128]{2,1,0:T(8,128)S(1)}) custom-call(bf16[72,4096]{1,0:T(8,128)(2,1)S(1)} %get-tuple-element.44.held_ref, f32[16,16]{1,0:T(8,128)S(1)} %get-tuple-element.43.tables_ref), custom_call_target="tpu_custom_call" | custom-call | tf_op jit(solution)/shard_map/pallas_call | solution.py:296
  35.6 0.0 collective-permute-done.halo_ref
  35.6 0.7 %shard_map.75 = f32[64,64,128]{2,1,0:T(8,128)} custom-call(f32[64,64,128]{2,1,0:T(8,128)} %get-tuple-element.45._, f32[64,8,128]{2,1,0:T(8,128)S(1)} %get-tuple-element.46.strip_ref, bf16[64,8,128]{2,1,0:T(8,128)(2,1)S(1)} %collective-permute-done.halo_ref), custom_call_target="tpu_custom_call", output_to_operand_aliasing={{}: (0, {})} | custom-call | tf_op jit(solution)/shard_map/pallas_call | solution.py:325
Async XLA Ops:
  2.2 22.5 %all-to-all-start.1 = ((bf16[16,48,128]{2,1,0:T(8,128)(2,1)}), bf16[16,48,128]{2,1,0:T(8,128)(2,1)S(1)}, u32[]{:S(2)}, u32[]{:S(2)}) async-start(bf16[16,48,128]{2,1,0:T(8,128)(2,1)} %get-tuple-element.42), calls=%async_computation.1 | async-start | bytes 393216 | tf_op jit(solution)/shard_map/all_to_all | solution.py:347
  27.8 7.7 %collective-permute-start = (bf16[64,8,128]{2,1,0:T(8,128)(2,1)S(1)}, bf16[64,8,128]{2,1,0:T(8,128)(2,1)S(1)}, u32[]{:S(2)}, u32[]{:S(2)}) collective-permute-start(bf16[64,8,128]{2,1,0:T(8,128)(2,1)S(1)} %get-tuple-element.47), channel_id=1, source_target_pairs={{0,32},{32,64},{64,96},{96,128},{128,160},{160,192},{192,224},{1,3... | collective-permute-start | bytes 393224 | tf_op jit(solution)/shard_map/ppermute | solution.py:359

commit v4 on v3

--- a/solution.py
+++ b/solution.py
@@ -93,11 +93,9 @@
     place = lax.broadcasted_iota(jnp.int32, (META, LANES), 1)
     per_row = LANES // (2 * META)
     for d in range(n_dst):
-        held = jnp.minimum(total[d : d + 1, :], float(cap))
-        coarse = jnp.floor(held / 64.0)
+        eights = jnp.floor((jnp.minimum(total[d : d + 1, :], float(cap)) + (META - 1)) / META)
         row = jnp.where(place == 4, over, 0.0)
-        row = jnp.where(place == 5, coarse, row)
-        row = jnp.where(place == 6, held - 64.0 * coarse, row)
+        row = jnp.where(place == 5, eights, row)
         for g in range(half // META):
             at = d * half + g * META
             part = sent[at : at + META, LANES:]
@@ -140,30 +138,25 @@
     return result
 
 
-def v_weights(tags, plane, kern_v, facet):
-    start = tags[1:2, :] + GV * (tags[2:3, :] - facet)
-    wide = spread(tap_rows(kern_v, plane), start, 0, GV)
-    high = wide.astype(BF16)
-    low = (wide - high.astype(F32)).astype(BF16)
-    return jnp.concatenate([high, low], axis=0)
-
-
 def weighted(vis, ku):
     chans, span, lanes = vis.shape[0], ku.shape[0], vis.shape[1]
     full = vis[:, None, :] * ku[None, :, :]
     return full.reshape(chans * span, lanes).astype(BF16)
 
 
-def border_kernel(half, chans, msgs_ref, tables_ref, held_ref, halo_ref, rows_s, acc):
+def border_kernel(half, chans, msgs_ref, tables_ref, held_ref, halo_ref, over_ref, *rest):
+    rows_s, acc = rest[-2:]
     n_src = msgs_ref.shape[0]
     facet = lax.axis_index("fv")
     lane = lax.broadcasted_iota(jnp.int32, (META, LANES), 1)
     per_row = LANES // (2 * META)
 
     lengths = []
+    over = jnp.zeros((META, LANES), F32)
     for src in range(n_src):
         tags = msgs_ref[src, half : half + META, :].astype(F32)
-        lengths.append((64.0 * tags[0, 5] + tags[0, 6]).astype(jnp.int32))
+        over = over + tags
+        lengths.append(tags[0, 5].astype(jnp.int32) * META)
 
     def rows_of(src, upper):
         tags = msgs_ref[src, half:, :].astype(F32)
@@ -178,6 +171,8 @@
             parts.append(jnp.where(lane < chans, vis[g * META : (g + 1) * META], tag))
         return jnp.concatenate(parts, axis=0)
 
+    over = over[0, 4].astype(jnp.int32)
+    over_ref[0, 0] = over
     offset = 0
     for src in range(n_src):
         rows_s[pl.ds(offset, half), :] = rows_of(src, 0)
@@ -186,58 +181,85 @@
         def _(src=src, offset=offset):
             rows_s[pl.ds(offset + half, half), :] = rows_of(src, 1)
 
-        offset = offset + lengths[src]
+        offset = pl.multiple_of(offset + lengths[src], META)
     rows_s[pl.ds(offset, KT), :] = jnp.zeros((KT, LANES), F32)
     tiles = jnp.maximum((offset + KT - 1) // KT, 1)
-    acc[...] = jnp.zeros_like(acc)
     kern_u, kern_v = tables_ref[:TAPS, :], tables_ref[TAPS:, :]
     tag_id = lax.broadcasted_iota(jnp.int32, (META, KT), 0)
-
-    def step(k, _):
+    kept = jnp.where(over > 0, 0, tiles).astype(F32)
+
+    def operands(k):
         cols = pl.ds(pl.multiple_of(k * KT, KT), KT)
         turned = rows_s[cols, :].T
         vis, tags = turned[:chans], turned[chans : chans + META]
         held_ref[:chans, cols] = vis.astype(BF16)
-        held_ref[chans:, cols] = jnp.where(tag_id == META - 1, tiles.astype(F32), tags).astype(BF16)
+        held_ref[chans:, cols] = jnp.where(tag_id == META - 1, kept, tags).astype(BF16)
         tags = tags.astype(jnp.int32)
         plane = tags[3:4, :]
         ku = spread(tap_rows(kern_u, plane), tags[0:1, :], GU, TAPS)
         left = weighted(vis, ku.astype(BF16).astype(F32))
-        right = v_weights(tags, plane, kern_v, facet)
-        acc[...] += lax.dot_general(left, right, NT, preferred_element_type=F32)
-        return 0
-
-    lax.fori_loop(0, tiles, step, 0)
-    halo_ref[...] = (acc[:, :GV] + acc[:, GV:]).reshape(chans, TAPS, GV).astype(BF16)
-
-
-def border(half, chans, msgs, tables, width):
+        start = tags[1:2, :] + GV * (tags[2:3, :] - facet)
+        return left, spread(tap_rows(kern_v, plane), start, 0, GV).astype(BF16)
+
+    def emit(total):
+        halo_ref[...] = total.reshape(chans, TAPS, GV).astype(BF16)
+
+    for n in (1, 2, 3):
+
+        @pl.when(tiles == n)
+        def _(n=n):
+            pairs = [operands(k) for k in range(n)]
+            left = jnp.concatenate([p[0] for p in pairs], axis=1)
+            right = jnp.concatenate([p[1] for p in pairs], axis=1)
+            emit(lax.dot_general(left, right, NT, preferred_element_type=F32))
+
+    @pl.when(tiles > 3)
+    def _():
+        acc[...] = jnp.zeros_like(acc)
+
+        def step(k, _):
+            left, right = operands(k)
+            acc[...] += lax.dot_general(left, right, NT, preferred_element_type=F32)
+            return 0
+
+        lax.fori_loop(0, tiles, step, 0)
+        emit(acc[...])
+
+
+def border(half, chans, msgs, tables, width, spare):
     vmem = pl.BlockSpec(memory_space=pltpu.VMEM)
     return pl.pallas_call(
         functools.partial(border_kernel, half, chans),
         out_shape=(
             jax.ShapeDtypeStruct((chans + META, width), BF16),
             jax.ShapeDtypeStruct((chans, TAPS, GV), BF16),
-        ),
+            jax.ShapeDtypeStruct((1, 1), jnp.int32),
+        )
+        + (jax.ShapeDtypeStruct((chans + META, width), BF16),) * spare,
         in_specs=[vmem, vmem],
-        out_specs=(vmem, vmem),
+        out_specs=(vmem, vmem, pl.BlockSpec(memory_space=pltpu.SMEM))
+        + (pl.BlockSpec(memory_space=pl.ANY),) * spare,
         scratch_shapes=[
             pltpu.VMEM((width + 2 * KT, LANES), F32),
-            pltpu.VMEM((chans * TAPS, 2 * GV), F32),
+            pltpu.VMEM((chans * TAPS, GV), F32),
         ],
         compiler_params=pltpu.CompilerParams(vmem_limit_bytes=12 << 20),
     )(msgs, tables)
 
 
-def main_kernel(step_chans, held_ref, tables_ref, out_ref, strip_ref, grid_s, ku_s, kv_s, acc, sems):
+def main_kernel(
+    step_chans, held_ref, other_ref, tables_ref, out_ref, strip_ref, other_s, grid_s, ku_s, kv_s, acc, sems, other_sem
+):
     chans = held_ref.shape[0] - META
     facet = lax.axis_index("fv")
     kern_u, kern_v = tables_ref[:TAPS, :], tables_ref[TAPS:, :]
-    tiles = held_ref[chans:, :LANES].astype(F32)[META - 1, 0].astype(jnp.int32)
-
-    def prepare(k):
+
+    def tiles_of(ref):
+        return ref[chans:, :LANES].astype(F32)[META - 1, 0].astype(jnp.int32)
+
+    def prepare(ref, k):
         cols = pl.ds(pl.multiple_of(k * KT, KT), KT)
-        tags = held_ref[chans:, cols].astype(F32).astype(jnp.int32)
+        tags = ref[chans:, cols].astype(F32).astype(jnp.int32)
         plane = tags[3:4, :]
         ku_s[:, cols] = spread(tap_rows(kern_u, plane), tags[0:1, :], 0, GU).astype(BF16)
         start = tags[1:2, :] + GV * (tags[2:3, :] - facet)
@@ -246,8 +268,8 @@
         kv_s[cols, :GV] = high
         kv_s[cols, GV:] = (wide - high.astype(F32)).astype(BF16)
 
-    def product(first, cols):
-        vis = held_ref[pl.ds(first, step_chans), cols].astype(F32)
+    def product(ref, first, cols):
+        vis = ref[pl.ds(first, step_chans), cols].astype(F32)
         left = weighted(vis, ku_s[:, cols].astype(F32))
         return jnp.dot(left, kv_s[cols, :], preferred_element_type=F32)
 
@@ -263,33 +285,45 @@
         copy_out(i).start()
 
     steps = chans // step_chans
+    tiles = tiles_of(held_ref)
+
+    def any_count(ref, count):
+        lax.fori_loop(0, count, lambda k, _: (prepare(ref, k), 0)[1], 0)
+        for i in range(steps):
+            acc[...] = jnp.zeros_like(acc)
+
+            def step(k, _, i=i):
+                acc[...] += product(ref, i * step_chans, pl.ds(pl.multiple_of(k * KT, KT), KT))
+                return 0
+
+            lax.fori_loop(0, count, step, 0)
+            emit(i, acc[...])
+
     for n in (1, 2, 3):
 
         @pl.when(tiles == n)
         def _(n=n):
             for k in range(n):
-                prepare(k)
+                prepare(held_ref, k)
             for i in range(steps):
-                emit(i, product(i * step_chans, pl.ds(0, n * KT)))
+                emit(i, product(held_ref, i * step_chans, pl.ds(0, n * KT)))
 
     @pl.when(tiles > 3)
     def _():
-        lax.fori_loop(0, tiles, lambda k, _: (prepare(k), 0)[1], 0)
-        for i in range(steps):
-            acc[...] = jnp.zeros_like(acc)
-
-            def step(k, _, i=i):
-                acc[...] += product(i * step_chans, pl.ds(pl.multiple_of(k * KT, KT), KT))
-                return 0
-
-            lax.fori_loop(0, tiles, step, 0)
-            emit(i, acc[...])
+        any_count(held_ref, tiles)
+
+    @pl.when(tiles == 0)
+    def _():
+        fetch = pltpu.make_async_copy(other_ref, other_s, other_sem)
+        fetch.start()
+        fetch.wait()
+        any_count(other_s, tiles_of(other_s))
 
     for i in range(steps):
         copy_out(i).wait()
 
 
-def main(held, tables, step_chans=16):
+def main(held, other, tables, step_chans=16):
     depth, width = held.shape
     chans = depth - META
     vmem = pl.BlockSpec(memory_space=pltpu.VMEM)
@@ -299,21 +333,24 @@
             jax.ShapeDtypeStruct((chans, GU, GV), F32),
             jax.ShapeDtypeStruct((chans, TAPS, GV), F32),
         ),
-        in_specs=[vmem, vmem],
+        in_specs=[vmem, pl.BlockSpec(memory_space=pl.ANY), vmem],
         out_specs=(pl.BlockSpec(memory_space=pl.ANY), vmem),
         scratch_shapes=[
+            pltpu.VMEM(held.shape, BF16),
             pltpu.VMEM((chans, GU, GV), F32),
             pltpu.VMEM((GU, width), BF16),
             pltpu.VMEM((width, 2 * GV), BF16),
             pltpu.VMEM((step_chans * GU, 2 * GV), F32),
             pltpu.SemaphoreType.DMA((chans // step_chans,)),
+            pltpu.SemaphoreType.DMA(()),
         ],
         compiler_params=pltpu.CompilerParams(vmem_limit_bytes=18 << 20),
-    )(held, tables)
+    )(held, other, tables)
 
 
 def join_kernel(_, strip_ref, halo_ref, out_ref, total, sem):
-    total[...] = strip_ref[...] + halo_ref[...].astype(F32)
+    below = jnp.where(lax.axis_index("fu") > 0, halo_ref[...].astype(F32), 0.0)
+    total[...] = strip_ref[...] + below
     copy = pltpu.make_async_copy(total, out_ref.at[:, pl.ds(0, TAPS), :], sem)
     copy.start()
     copy.wait()
@@ -347,17 +384,14 @@
         return lax.all_to_all(sent, "fv", 0, 0), tables
 
     msgs, tables = exchange(usual_half)
-    over = jnp.any(msgs[:, usual_half, 4] > 0)
-
-    def whole():
-        return border(rows // 2, chans, exchange(rows // 2)[0], tables, width)
-
-    def usual():
-        return border(usual_half, chans, msgs, tables, width)
-
-    held, halo = lax.cond(over, whole, usual)
-    came = lax.ppermute(halo, "fu", [(i, i + 1) for i in range(n_fu - 1)])
-    grid, strip = main(held, tables)
+    held, halo, over, other = border(usual_half, chans, msgs, tables, width, 1)
+
+    def whole(_):
+        return border(rows // 2, chans, exchange(rows // 2)[0], tables, width, 0)
+
+    other, halo, _ = lax.while_loop(lambda state: state[2][0, 0] > 0, whole, (other, halo, over))
+    came = lax.ppermute(halo, "fu", [(i, (i + 1) % n_fu) for i in range(n_fu)])
+    grid, strip = main(held, other, tables)
     return join(grid, strip, came)
 
 

time: 36.6 us -> 33.9 us (0.926)
  blocking collectives: 0 us -> 22.3 us
  starting transfers between devices: 17.3 us -> 3.68 us
  waiting for transfers between devices: 10.8 us -> 0.14 us
  other arithmetic: 0.72 us -> 0 us
  loops' own time: 0.02 us -> 0.65 us
  between operations: 0.69 us -> 0.19 us
    all_to_all x0 -> x1, blocking collectives: none -> 22.3 us  [exchange(): return (lax.all_to_all(sent, 'fv', 0, 0), tables)]
    all_to_all x1 -> x0, starting transfers between devices: 11.7 us -> none  [exchange(): return (lax.all_to_all(sent, 'fv', 0, 0), tables)]
    all_to_all x1 -> x0, waiting for transfers between devices: 10.8 us -> none  [exchange(): return (lax.all_to_all(sent, 'fv', 0, 0), tables)]
    ppermute x1, starting transfers between devices: 5.58 us -> 3.68 us  [per_device(): came = lax.ppermute(halo, 'fu', [(i, (i + 1) % n_fu) for i in range(n_fu)])]
    reduce_or x1 -> x0, other arithmetic: 0.72 us -> none  [per_device(): over = jnp.any(msgs[:, usual_half, 4] > 0)]
    pallas_call x1, Pallas kernels: 2.16 us -> 1.48 us  [pack(): pl.pallas_call(functools.partial(pack_kernel, half, n_dst), out_shape=(ja...]
    another operation x1, loops' own time: 0.02 us -> 0.65 us  [per_device(): lax.while_loop(lambda state: state[2][0, 0] > 0, whole, (other, halo, over))]
    pallas_call x1, Pallas kernels: 1.76 us -> 2.33 us  [border(): pl.pallas_call(functools.partial(border_kernel, half, chans), out_shape=(...]
  transfers between devices with their start and end apart: 2 -> 1, of which waited for: 1 -> 1; matrix products, arithmetic and copies ran while one was open for 0% -> 0% of each run, Pallas kernels for 6% -> 6%
where the time goes in v4:
time: 33.9 us; the launch traced here: 33.6 us
  blocking collectives  22.3 us (66%)
  Pallas kernels  6.67 us (20%)
  starting transfers between devices  3.68 us (11%)
  loops' own time  0.65 us (2%)
    all_to_all x1, blocking collectives, exchange(): return (lax.all_to_all(sent, 'fv', 0, 0), tables)  22.3 us
    ppermute x1, starting transfers between devices, per_device(): came = lax.ppermute(halo, 'fu', [(i, (i + 1) % n_fu) for i in range(n_fu)])  3.68 us
    pallas_call x1, Pallas kernels, border(): pl.pallas_call(functools.partial(border_kernel, half, chans), out_shape=(...  2.33 us
    pallas_call x1, Pallas kernels, main(): pl.pallas_call(functools.partial(main_kernel, step_chans), out_shape=(jax...  2.12 us
    pallas_call x1, Pallas kernels, pack(): pl.pallas_call(functools.partial(pack_kernel, half, n_dst), out_shape=(ja...  1.48 us
    pallas_call x1, Pallas kernels, join(): pl.pallas_call(join_kernel, out_shape=jax.ShapeDtypeStruct(grid.shape, gr...  0.74 us
  transfers between devices with their start and end apart: 1, of which 1 were waited for; matrix products, arithmetic and copies ran while one was open for 0% of the time, Pallas kernels for 6%

profile of v4, /device:TPU:1, one launch (start us, length us, event | category | flops | bytes accessed | tf_op | source)
XLA Modules:
  0.0 33.6 jit_solution(3560041807395474424)
XLA Ops:
  0.0 1.5 %shard_map.73 = (bf16[16,48,128]{2,1,0:T(8,128)(2,1)S(1)}, f32[16,16]{1,0:T(8,128)S(1)}) custom-call(s32[1,384]{1,0:T(1,128)} %u_ref.1, s32[1,384]{1,0:T(1,128)} %v_ref.1, s32[1,384]{1,0:T(1,128)} %w_ref.1, s32[1,3]{1,0:T(1,128)} %counts_ref.1, bf16[64,384]{1,0:T(8,128)(2,1)} %bitcast.6, f32[8,16]{1,0:T(8,128)} %bitcast.8, f32[8,16]{1,0:T(8,128)} %bitcast.10), custom_call_target="tpu_custom_call" | custom-call | tf_op jit(solution)/shard_map/pallas_call | solution.py:113
  1.5 22.3 %all_to_all.10.msgs_ref = bf16[16,48,128]{2,1,0:T(8,128)(2,1)S(1)} all-to-all(bf16[16,48,128]{2,1,0:T(8,128)(2,1)S(1)} %get-tuple-element.72), channel_id=1, replica_groups=mesh['fu'=8,'fv'=16,'ch'=2] {'fv'}, dimensions={0} | all-to-all | bytes 393216 | tf_op jit(solution)/shard_map/all_to_all | solution.py:384
  23.8 2.3 %shard_map.74 = (bf16[72,4096]{1,0:T(8,128)(2,1)S(1)}, bf16[64,8,128]{2,1,0:T(8,128)(2,1)}, s32[1,1]{1,0:T(1,128)}, bf16[72,4096]{1,0:T(8,128)(2,1)}) custom-call(bf16[16,48,128]{2,1,0:T(8,128)(2,1)S(1)} %all_to_all.10.msgs_ref, f32[16,16]{1,0:T(8,128)S(1)} %get-tuple-element.125.tables_ref), custom_call_target="tpu_custom_call" | custom-call | tf_op jit(solution)/shard_map/pallas_call | solution.py:231
  26.1 0.7 %while.11 = (bf16[72,4096]{1,0:T(8,128)(2,1)}, bf16[64,8,128]{2,1,0:T(8,128)(2,1)}, s32[1,1]{1,0:T(1,128)}, f32[16,8]{0,1:T(8,128)}, f32[16,8]{0,1:T(8,128)}, /*...) while((bf16[72,4096]{1,0:T(8,128)(2,1)}, ...), condition=%region_1.0_spmd, body=%region_0.0_spmd | while | flops 1 | bytes 1769569 | solution.py:392
  26.8 3.7 %collective-permute-start = (bf16[64,8,128]{2,1,0:T(8,128)(2,1)}, bf16[64,8,128]{2,1,0:T(8,128)(2,1)S(1)}, u32[]{:S(2)}, u32[]{:S(2)}) collective-permute-start(bf16[64,8,128]{2,1,0:T(8,128)(2,1)} %get-tuple-element.81), channel_id=1, source_target_pairs={{0,32},{32,64},{64,96},{96,128},{128,160},{160,192},{192,224},{224... | collective-permute-start | bytes 393224 | tf_op jit(solution)/shard_map/ppermute | solution.py:393
  30.5 2.1 %shard_map.75 = (f32[64,64,128]{2,1,0:T(8,128)}, f32[64,8,128]{2,1,0:T(8,128)S(1)}) custom-call(bf16[72,4096]{1,0:T(8,128)(2,1)S(1)} %get-tuple-element.74.held_ref, bf16[72,4096]{1,0:T(8,128)(2,1)} %get-tuple-element.78.other_ref, f32[16,16]{1,0:T(8,128)S(1)} %get-tuple-element.149), custom_call_target="tpu_custom_call" | custom-call | tf_op jit(solution)/shard_map/pallas_call | solution.py:330
  32.6 0.1 collective-permute-done.halo_ref
  32.7 0.7 %shard_map.76 = f32[64,64,128]{2,1,0:T(8,128)} custom-call(f32[64,64,128]{2,1,0:T(8,128)} %get-tuple-element.79._, f32[64,8,128]{2,1,0:T(8,128)S(1)} %get-tuple-element.80.strip_ref, bf16[64,8,128]{2,1,0:T(8,128)(2,1)S(1)} %collective-permute-done.halo_ref), custom_call_target="tpu_custom_call", output_to_operand_aliasing={{}: (0, {})} | custom-call | tf_op jit(solution)/shard_map/pallas_call | solution.py:362
Async XLA Ops:
  26.8 5.9 %collective-permute-start = (bf16[64,8,128]{2,1,0:T(8,128)(2,1)}, bf16[64,8,128]{2,1,0:T(8,128)(2,1)S(1)}, u32[]{:S(2)}, u32[]{:S(2)}) collective-permute-start(bf16[64,8,128]{2,1,0:T(8,128)(2,1)} %get-tuple-element.81), channel_id=1, source_target_pairs={{0,32},{32,64},{64,96},{96,128},{128,160},{160,192},{192,224},{224... | collective-permute-start | bytes 393224 | tf_op jit(solution)/shard_map/ppermute | solution.py:393

commit v5 on v3

--- a/solution.py
+++ b/solution.py
@@ -42,17 +42,21 @@
     last = (v + (TAPS - 1)) // GV
     dst = lax.broadcasted_iota(jnp.int32, (n_dst, rows), 0)
     member = ((dst == first) | (dst == last)) & live
-    member_f = member.astype(F32)
+    edge = member & (u % GU > GU - TAPS)
+    plain_f = (member & jnp.logical_not(edge)).astype(F32)
+    edge_f = edge.astype(F32)
     before = lax.broadcasted_iota(jnp.int32, (rows, rows), 0) < lax.broadcasted_iota(
         jnp.int32, (rows, rows), 1
     )
     rank = jnp.dot(
-        member_f.astype(BF16),
+        jnp.concatenate([edge_f, plain_f], axis=0).astype(BF16),
         before.astype(F32).astype(BF16),
         preferred_element_type=F32,
     )
+    edges = jnp.sum(edge_f, axis=1, keepdims=True)
+    total = edges + jnp.sum(plain_f, axis=1, keepdims=True)
+    rank = jnp.where(edge, rank[:n_dst], rank[n_dst:] + edges)
     rank = jnp.where(member, rank.astype(jnp.int32), -1)
-    total = jnp.sum(member_f, axis=1, keepdims=True)
     over = (jnp.max(total, axis=0, keepdims=True) > cap).astype(F32)
     tags = jnp.concatenate(
         [
@@ -93,11 +97,10 @@
     place = lax.broadcasted_iota(jnp.int32, (META, LANES), 1)
     per_row = LANES // (2 * META)
     for d in range(n_dst):
-        held = jnp.minimum(total[d : d + 1, :], float(cap))
-        coarse = jnp.floor(held / 64.0)
+        eights = jnp.floor((jnp.minimum(total[d : d + 1, :], float(cap)) + (META - 1)) / META)
         row = jnp.where(place == 4, over, 0.0)
-        row = jnp.where(place == 5, coarse, row)
-        row = jnp.where(place == 6, held - 64.0 * coarse, row)
+        row = jnp.where(place == 5, eights, row)
+        row = jnp.where(place == 6, jnp.floor((edges[d : d + 1, :] + (META - 1)) / META), row)
         for g in range(half // META):
             at = d * half + g * META
             part = sent[at : at + META, LANES:]
@@ -140,104 +143,171 @@
     return result
 
 
-def v_weights(tags, plane, kern_v, facet):
-    start = tags[1:2, :] + GV * (tags[2:3, :] - facet)
-    wide = spread(tap_rows(kern_v, plane), start, 0, GV)
-    high = wide.astype(BF16)
-    low = (wide - high.astype(F32)).astype(BF16)
-    return jnp.concatenate([high, low], axis=0)
-
-
 def weighted(vis, ku):
     chans, span, lanes = vis.shape[0], ku.shape[0], vis.shape[1]
     full = vis[:, None, :] * ku[None, :, :]
     return full.reshape(chans * span, lanes).astype(BF16)
 
 
-def border_kernel(half, chans, msgs_ref, tables_ref, held_ref, halo_ref, rows_s, acc):
-    n_src = msgs_ref.shape[0]
-    facet = lax.axis_index("fv")
+def merged_rows(half, chans, msgs_ref, src, upper, groups):
     lane = lax.broadcasted_iota(jnp.int32, (META, LANES), 1)
     per_row = LANES // (2 * META)
-
+    parts = []
+    for g in groups:
+        at = half + META * (g // per_row)
+        vis = msgs_ref[src, g * META : (g + 1) * META, :].astype(F32)
+        tag = msgs_ref[src, at : at + META, :].astype(F32)
+        if upper:
+            vis = pltpu.roll(vis, LANES // 2, 1)
+        shift = (chans - 2 * META * (g % per_row) - META * upper) % LANES
+        parts.append(jnp.where(lane < chans, vis, pltpu.roll(tag, shift, 1)))
+    return jnp.concatenate(parts, axis=0)
+
+
+def gather_rows(half, chans, msgs_ref, rows_s):
+    n_src = msgs_ref.shape[0]
+    groups = range(half // META)
     lengths = []
     for src in range(n_src):
         tags = msgs_ref[src, half : half + META, :].astype(F32)
-        lengths.append((64.0 * tags[0, 5] + tags[0, 6]).astype(jnp.int32))
-
-    def rows_of(src, upper):
-        tags = msgs_ref[src, half:, :].astype(F32)
-        vis = msgs_ref[src, :half, :].astype(F32)
-        if upper:
-            vis = pltpu.roll(vis, LANES // 2, 1)
-        parts = []
-        for g in range(half // META):
-            at = META * (g // per_row)
-            shift = (chans - 2 * META * (g % per_row) - META * upper) % LANES
-            tag = pltpu.roll(tags[at : at + META], shift, 1)
-            parts.append(jnp.where(lane < chans, vis[g * META : (g + 1) * META], tag))
-        return jnp.concatenate(parts, axis=0)
-
+        lengths.append(tags[0, 5].astype(jnp.int32) * META)
     offset = 0
     for src in range(n_src):
-        rows_s[pl.ds(offset, half), :] = rows_of(src, 0)
+        rows_s[pl.ds(offset, half), :] = merged_rows(half, chans, msgs_ref, src, 0, groups)
 
         @pl.when(lengths[src] > half)
         def _(src=src, offset=offset):
-            rows_s[pl.ds(offset + half, half), :] = rows_of(src, 1)
-
-        offset = offset + lengths[src]
+            rows_s[pl.ds(offset + half, half), :] = merged_rows(half, chans, msgs_ref, src, 1, groups)
+
+        offset = pl.multiple_of(offset + lengths[src], META)
     rows_s[pl.ds(offset, KT), :] = jnp.zeros((KT, LANES), F32)
-    tiles = jnp.maximum((offset + KT - 1) // KT, 1)
+    return jnp.maximum((offset + KT - 1) // KT, 1)
+
+
+def turn_tile(chans, rows_s, held, tiles, k):
+    cols = pl.ds(pl.multiple_of(k * KT, KT), KT)
+    turned = rows_s[cols, :].T
+    tag_id = lax.broadcasted_iota(jnp.int32, (META, KT), 0)
+    tags = turned[chans : chans + META]
+    held[:chans, cols] = turned[:chans].astype(BF16)
+    held[chans:, cols] = jnp.where(tag_id == META - 1, tiles.astype(F32), tags).astype(BF16)
+
+
+def border_product(chans, block, tables_ref):
+    kern_u, kern_v = tables_ref[:TAPS, :], tables_ref[TAPS:, :]
+    turned = block.T
+    tags = turned[chans : chans + META].astype(jnp.int32)
+    plane = tags[3:4, :]
+    ku = spread(tap_rows(kern_u, plane), tags[0:1, :], GU, TAPS)
+    left = weighted(turned[:chans], ku.astype(BF16).astype(F32))
+    start = tags[1:2, :] + GV * (tags[2:3, :] - lax.axis_index("fv"))
+    right = spread(tap_rows(kern_v, plane), start, 0, GV).astype(BF16)
+    return lax.dot_general(left, right, NT, preferred_element_type=F32)
+
+
+def sum_of_tags(half, msgs_ref):
+    total = jnp.zeros((META, LANES), F32)
+    for src in range(msgs_ref.shape[0]):
+        total = total + msgs_ref[src, half : half + META, :].astype(F32)
+    return total
+
+
+def whole_kernel(half, chans, msgs_ref, tables_ref, held_ref, halo_ref, over_ref, rows_s, acc):
+    tiles = gather_rows(half, chans, msgs_ref, rows_s)
     acc[...] = jnp.zeros_like(acc)
-    kern_u, kern_v = tables_ref[:TAPS, :], tables_ref[TAPS:, :]
-    tag_id = lax.broadcasted_iota(jnp.int32, (META, KT), 0)
 
     def step(k, _):
-        cols = pl.ds(pl.multiple_of(k * KT, KT), KT)
-        turned = rows_s[cols, :].T
-        vis, tags = turned[:chans], turned[chans : chans + META]
-        held_ref[:chans, cols] = vis.astype(BF16)
-        held_ref[chans:, cols] = jnp.where(tag_id == META - 1, tiles.astype(F32), tags).astype(BF16)
-        tags = tags.astype(jnp.int32)
-        plane = tags[3:4, :]
-        ku = spread(tap_rows(kern_u, plane), tags[0:1, :], GU, TAPS)
-        left = weighted(vis, ku.astype(BF16).astype(F32))
-        right = v_weights(tags, plane, kern_v, facet)
-        acc[...] += lax.dot_general(left, right, NT, preferred_element_type=F32)
+        turn_tile(chans, rows_s, held_ref, tiles, k)
+        block = rows_s[pl.ds(pl.multiple_of(k * KT, KT), KT), :]
+        acc[...] += border_product(chans, block, tables_ref)
         return 0
 
     lax.fori_loop(0, tiles, step, 0)
-    halo_ref[...] = (acc[:, :GV] + acc[:, GV:]).reshape(chans, TAPS, GV).astype(BF16)
-
-
-def border(half, chans, msgs, tables, width):
+    halo_ref[...] = acc[...].reshape(chans, TAPS, GV).astype(BF16)
+    over_ref[0, 0] = 0
+
+
+def early():
+    return lax.axis_index("fu") % 2 == 1
+
+
+def usual_kernel(half, chans, msgs_ref, tables_ref, held_ref, halo_ref, over_ref, other_ref, rows_s, acc):
+    n_src = msgs_ref.shape[0]
+    groups = half // META
+    over_ref[0, 0] = sum_of_tags(half, msgs_ref)[0, 4].astype(jnp.int32)
+    most = jnp.zeros((META, LANES), F32)
+    for src in range(n_src):
+        most = jnp.maximum(most, msgs_ref[src, half : half + META, :].astype(F32))
+    chunks = most[0, 6].astype(jnp.int32)
+
+    def chunk(c):
+        upper, g = c // groups, c % groups
+        block = [merged_rows(half, chans, msgs_ref, src, upper, [g]) for src in range(n_src)]
+        return border_product(chans, jnp.concatenate(block, axis=0), tables_ref)
+
+    def emit(total):
+        halo_ref[...] = total.reshape(chans, TAPS, GV).astype(BF16)
+
+    @pl.when(chunks <= 1)
+    def _():
+        emit(chunk(0))
+
+    @pl.when(chunks > 1)
+    def _():
+        acc[...] = chunk(0) + chunk(1)
+        for c in range(2, 2 * groups):
+
+            @pl.when(chunks > c)
+            def _(c=c):
+                acc[...] += chunk(c)
+
+        emit(acc[...])
+
+    @pl.when(early())
+    def _():
+        tiles = gather_rows(half, chans, msgs_ref, rows_s)
+        lax.fori_loop(0, tiles, lambda k, _: (turn_tile(chans, rows_s, held_ref, tiles, k), 0)[1], 0)
+
+
+def border(half, chans, msgs, tables, width, usual):
     vmem = pl.BlockSpec(memory_space=pltpu.VMEM)
+    whole = jax.ShapeDtypeStruct((chans + META, width), BF16)
+    most = width
+    if usual:
+        most = -(-2 * half * msgs.shape[0] // KT) * KT
     return pl.pallas_call(
-        functools.partial(border_kernel, half, chans),
+        functools.partial(usual_kernel if usual else whole_kernel, half, chans),
         out_shape=(
-            jax.ShapeDtypeStruct((chans + META, width), BF16),
+            jax.ShapeDtypeStruct((chans + META, most), BF16),
             jax.ShapeDtypeStruct((chans, TAPS, GV), BF16),
-        ),
+            jax.ShapeDtypeStruct((1, 1), jnp.int32),
+        )
+        + (whole,) * usual,
         in_specs=[vmem, vmem],
-        out_specs=(vmem, vmem),
+        out_specs=(vmem, vmem, pl.BlockSpec(memory_space=pltpu.SMEM))
+        + (pl.BlockSpec(memory_space=pl.ANY),) * usual,
         scratch_shapes=[
-            pltpu.VMEM((width + 2 * KT, LANES), F32),
-            pltpu.VMEM((chans * TAPS, 2 * GV), F32),
+            pltpu.VMEM((most + 2 * KT, LANES), F32),
+            pltpu.VMEM((chans * TAPS, GV), F32),
         ],
         compiler_params=pltpu.CompilerParams(vmem_limit_bytes=12 << 20),
     )(msgs, tables)
 
 
-def main_kernel(step_chans, held_ref, tables_ref, out_ref, strip_ref, grid_s, ku_s, kv_s, acc, sems):
-    chans = held_ref.shape[0] - META
+def main_kernel(
+    half, step_chans, msgs_ref, held_ref, other_ref, tables_ref, out_ref, strip_ref,
+    held_s, rows_s, grid_s, ku_s, kv_s, acc, sems, other_sem, tiles_s
+):
+    chans = held_s.shape[0] - META
     facet = lax.axis_index("fv")
     kern_u, kern_v = tables_ref[:TAPS, :], tables_ref[TAPS:, :]
-    tiles = held_ref[chans:, :LANES].astype(F32)[META - 1, 0].astype(jnp.int32)
+
+    def tiles_of(ref):
+        return ref[chans:, :LANES].astype(F32)[META - 1, 0].astype(jnp.int32)
 
     def prepare(k):
         cols = pl.ds(pl.multiple_of(k * KT, KT), KT)
-        tags = held_ref[chans:, cols].astype(F32).astype(jnp.int32)
+        tags = held_s[chans:, cols].astype(F32).astype(jnp.int32)
         plane = tags[3:4, :]
         ku_s[:, cols] = spread(tap_rows(kern_u, plane), tags[0:1, :], 0, GU).astype(BF16)
         start = tags[1:2, :] + GV * (tags[2:3, :] - facet)
@@ -247,7 +317,7 @@
         kv_s[cols, GV:] = (wide - high.astype(F32)).astype(BF16)
 
     def product(first, cols):
-        vis = held_ref[pl.ds(first, step_chans), cols].astype(F32)
+        vis = held_s[pl.ds(first, step_chans), cols].astype(F32)
         left = weighted(vis, ku_s[:, cols].astype(F32))
         return jnp.dot(left, kv_s[cols, :], preferred_element_type=F32)
 
@@ -263,6 +333,34 @@
         copy_out(i).start()
 
     steps = chans // step_chans
+    over = sum_of_tags(half, msgs_ref)[0, 4] > 0.0
+
+    @pl.when(over)
+    def _():
+        fetch = pltpu.make_async_copy(other_ref, held_s, other_sem)
+        fetch.start()
+        fetch.wait()
+        tiles_s[0] = tiles_of(held_s)
+
+    @pl.when(jnp.logical_not(over) & early())
+    def _():
+        tiles = tiles_of(held_ref)
+        tiles_s[0] = tiles
+
+        def copy_tile(k, _):
+            cols = pl.ds(pl.multiple_of(k * KT, KT), KT)
+            held_s[:, cols] = held_ref[:, cols]
+            return 0
+
+        lax.fori_loop(0, tiles, copy_tile, 0)
+
+    @pl.when(jnp.logical_not(over) & jnp.logical_not(early()))
+    def _():
+        tiles = gather_rows(half, chans, msgs_ref, rows_s)
+        tiles_s[0] = tiles
+        lax.fori_loop(0, tiles, lambda k, _: (turn_tile(chans, rows_s, held_s, tiles, k), 0)[1], 0)
+
+    tiles = tiles_s[0]
     for n in (1, 2, 3):
 
         @pl.when(tiles == n)
@@ -289,31 +387,36 @@
         copy_out(i).wait()
 
 
-def main(held, tables, step_chans=16):
-    depth, width = held.shape
+def main(half, msgs, held, other, tables, step_chans=16):
+    depth, width = other.shape
     chans = depth - META
     vmem = pl.BlockSpec(memory_space=pltpu.VMEM)
     return pl.pallas_call(
-        functools.partial(main_kernel, step_chans),
+        functools.partial(main_kernel, half, step_chans),
         out_shape=(
             jax.ShapeDtypeStruct((chans, GU, GV), F32),
             jax.ShapeDtypeStruct((chans, TAPS, GV), F32),
         ),
-        in_specs=[vmem, vmem],
+        in_specs=[vmem, vmem, pl.BlockSpec(memory_space=pl.ANY), vmem],
         out_specs=(pl.BlockSpec(memory_space=pl.ANY), vmem),
         scratch_shapes=[
+            pltpu.VMEM(other.shape, BF16),
+            pltpu.VMEM((held.shape[1] + 2 * KT, LANES), F32),
             pltpu.VMEM((chans, GU, GV), F32),
             pltpu.VMEM((GU, width), BF16),
             pltpu.VMEM((width, 2 * GV), BF16),
             pltpu.VMEM((step_chans * GU, 2 * GV), F32),
             pltpu.SemaphoreType.DMA((chans // step_chans,)),
+            pltpu.SemaphoreType.DMA(()),
+            pltpu.SMEM((1,), jnp.int32),
         ],
         compiler_params=pltpu.CompilerParams(vmem_limit_bytes=18 << 20),
-    )(held, tables)
+    )(msgs, held, other, tables)
 
 
 def join_kernel(_, strip_ref, halo_ref, out_ref, total, sem):
-    total[...] = strip_ref[...] + halo_ref[...].astype(F32)
+    below = jnp.where(lax.axis_index("fu") > 0, halo_ref[...].astype(F32), 0.0)
+    total[...] = strip_ref[...] + below
     copy = pltpu.make_async_copy(total, out_ref.at[:, pl.ds(0, TAPS), :], sem)
     copy.start()
     copy.wait()
@@ -347,17 +450,14 @@
         return lax.all_to_all(sent, "fv", 0, 0), tables
 
     msgs, tables = exchange(usual_half)
-    over = jnp.any(msgs[:, usual_half, 4] > 0)
-
-    def whole():
-        return border(rows // 2, chans, exchange(rows // 2)[0], tables, width)
-
-    def usual():
-        return border(usual_half, chans, msgs, tables, width)
-
-    held, halo = lax.cond(over, whole, usual)
-    came = lax.ppermute(halo, "fu", [(i, i + 1) for i in range(n_fu - 1)])
-    grid, strip = main(held, tables)
+    held, halo, over, other = border(usual_half, chans, msgs, tables, width, 1)
+
+    def whole(_):
+        return border(rows // 2, chans, exchange(rows // 2)[0], tables, width, 0)
+
+    other, halo, _ = lax.while_loop(lambda state: state[2][0, 0] > 0, whole, (other, halo, over))
+    came = lax.ppermute(halo, "fu", [(i, (i + 1) % n_fu) for i in range(n_fu)])
+    grid, strip = main(usual_half, msgs, held, other, tables)
     return join(grid, strip, came)
 
 

time: 36.6 us -> 32.7 us (0.89)
  blocking collectives: 0 us -> 22.3 us
  starting transfers between devices: 17.3 us -> 2.37 us
  waiting for transfers between devices: 10.8 us -> 0.01 us
  other arithmetic: 0.72 us -> 0 us
  loops' own time: 0.02 us -> 0.65 us
  between operations: 0.69 us -> 0.19 us
    all_to_all x0 -> x1, blocking collectives: none -> 22.3 us  [exchange(): return (lax.all_to_all(sent, 'fv', 0, 0), tables)]
    all_to_all x1 -> x0, starting transfers between devices: 11.7 us -> none  [exchange(): return (lax.all_to_all(sent, 'fv', 0, 0), tables)]
    all_to_all x1 -> x0, waiting for transfers between devices: 10.8 us -> none  [exchange(): return (lax.all_to_all(sent, 'fv', 0, 0), tables)]
    ppermute x1, starting transfers between devices: 5.58 us -> 2.37 us  [per_device(): came = lax.ppermute(halo, 'fu', [(i, (i + 1) % n_fu) for i in range(n_fu)])]
    pallas_call x2, Pallas kernels: 3.88 us -> 4.76 us  [the longest x1 2.49 us: border(): pl.pallas_call(functools.partial(usual_kernel if usual else whole_kernel,...]
    reduce_or x1 -> x0, other arithmetic: 0.72 us -> none  [per_device(): over = jnp.any(msgs[:, usual_half, 4] > 0)]
    pallas_call x1, Pallas kernels: 2.16 us -> 1.5 us  [pack(): pl.pallas_call(functools.partial(pack_kernel, half, n_dst), out_shape=(ja...]
    another operation x1, loops' own time: 0.02 us -> 0.65 us  [per_device(): lax.while_loop(lambda state: state[2][0, 0] > 0, whole, (other, halo, over))]
  transfers between devices with their start and end apart: 2 -> 1, of which waited for: 1 -> 0; matrix products, arithmetic and copies ran while one was open for 0% -> 0% of each run, Pallas kernels for 6% -> 7%
where the time goes in v5:
time: 32.7 us; the launch traced here: 32.5 us
  blocking collectives  22.3 us (68%)
  Pallas kernels  7.01 us (21%)
  starting transfers between devices  2.37 us (7%)
  loops' own time  0.65 us (2%)
    all_to_all x1, blocking collectives, exchange(): return (lax.all_to_all(sent, 'fv', 0, 0), tables)  22.3 us
    pallas_call x1, Pallas kernels, border(): pl.pallas_call(functools.partial(usual_kernel if usual else whole_kernel,...  2.49 us
    ppermute x1, starting transfers between devices, per_device(): came = lax.ppermute(halo, 'fu', [(i, (i + 1) % n_fu) for i in range(n_fu)])  2.37 us
    pallas_call x1, Pallas kernels, main(): pl.pallas_call(functools.partial(main_kernel, half, step_chans), out_shap...  2.27 us
    pallas_call x1, Pallas kernels, pack(): pl.pallas_call(functools.partial(pack_kernel, half, n_dst), out_shape=(ja...  1.5 us
    pallas_call x1, Pallas kernels, join(): pl.pallas_call(join_kernel, out_shape=jax.ShapeDtypeStruct(grid.shape, gr...  0.75 us
    another operation x1, loops' own time, per_device(): lax.while_loop(lambda state: state[2][0, 0] > 0, whole, (other, halo, over))  0.65 us
  transfers between devices with their start and end apart: 1, of which 0 were waited for; matrix products, arithmetic and copies ran while one was open for 0% of the time, Pallas kernels for 7%

profile of v5, /device:TPU:1, one launch (start us, length us, event | category | flops | bytes accessed | tf_op | source)
XLA Modules:
  0.0 32.5 jit_solution(2673424706834362043)
XLA Ops:
  0.0 1.5 %shard_map.73 = (bf16[16,48,128]{2,1,0:T(8,128)(2,1)S(1)}, f32[16,16]{1,0:T(8,128)S(1)}) custom-call(s32[1,384]{1,0:T(1,128)} %u_ref.1, s32[1,384]{1,0:T(1,128)} %v_ref.1, s32[1,384]{1,0:T(1,128)} %w_ref.1, s32[1,3]{1,0:T(1,128)} %counts_ref.1, bf16[64,384]{1,0:T(8,128)(2,1)} %bitcast.6, f32[8,16]{1,0:T(8,128)} %bitcast.8, f32[8,16]{1,0:T(8,128)} %bitcast.10), custom_call_target="tpu_custom_call" | custom-call | tf_op jit(solution)/shard_map/pallas_call | solution.py:118
  1.5 22.3 %all_to_all.10.msgs_ref = bf16[16,48,128]{2,1,0:T(8,128)(2,1)S(1)} all-to-all(bf16[16,48,128]{2,1,0:T(8,128)(2,1)S(1)} %get-tuple-element.72), channel_id=1, replica_groups=mesh['fu'=8,'fv'=16,'ch'=2] {'fv'}, dimensions={0} | all-to-all | bytes 393216 | tf_op jit(solution)/shard_map/all_to_all | solution.py:450
  23.8 2.5 %shard_map.74 = (bf16[72,1280]{1,0:T(8,128)(2,1)S(1)}, bf16[64,8,128]{2,1,0:T(8,128)(2,1)}, s32[1,1]{1,0:T(1,128)}, bf16[72,4096]{1,0:T(8,128)(2,1)}) custom-call(bf16[16,48,128]{2,1,0:T(8,128)(2,1)S(1)} %all_to_all.10.msgs_ref, f32[16,16]{1,0:T(8,128)S(1)} %get-tuple-element.125.tables_ref), custom_call_target="tpu_custom_call" | custom-call | tf_op jit(solution)/shard_map/pallas_call | solution.py:278
  26.3 0.7 %while.11 = (bf16[72,4096]{1,0:T(8,128)(2,1)}, bf16[64,8,128]{2,1,0:T(8,128)(2,1)}, s32[1,1]{1,0:T(1,128)}, f32[16,8]{0,1:T(8,128)}, f32[16,8]{0,1:T(8,128)}, /*...) while((bf16[72,4096]{1,0:T(8,128)(2,1)}, ...), condition=%region_1.0_spmd, body=%region_0.0_spmd | while | flops 1 | bytes 1769569 | solution.py:458
  27.0 2.4 %collective-permute-start = (bf16[64,8,128]{2,1,0:T(8,128)(2,1)}, bf16[64,8,128]{2,1,0:T(8,128)(2,1)S(1)}, u32[]{:S(2)}, u32[]{:S(2)}) collective-permute-start(bf16[64,8,128]{2,1,0:T(8,128)(2,1)} %get-tuple-element.81), channel_id=1, source_target_pairs={{0,32},{32,64},{64,96},{96,128},{128,160},{160,192},{192,224},{224... | collective-permute-start | bytes 393224 | tf_op jit(solution)/shard_map/ppermute | solution.py:459
  29.3 2.3 %shard_map.75 = (f32[64,64,128]{2,1,0:T(8,128)}, f32[64,8,128]{2,1,0:T(8,128)S(1)}) custom-call(bf16[16,48,128]{2,1,0:T(8,128)(2,1)S(1)} %all_to_all.10.msgs_ref, bf16[72,1280]{1,0:T(8,128)(2,1)S(1)} %get-tuple-element.74.held_ref, bf16[72,4096]{1,0:T(8,128)(2,1)} %get-tuple-element.78.other_ref, f32[16,16]{1,0:T(8,128)S(1)} %get-tuple-element.149), custom_call_target="tpu_custom_call" | custom-call | tf_op jit(solution)/shard_map/pallas_call | solution.py:394
  31.6 0.0 collective-permute-done.halo_ref
  31.6 0.8 %shard_map.76 = f32[64,64,128]{2,1,0:T(8,128)} custom-call(f32[64,64,128]{2,1,0:T(8,128)} %get-tuple-element.79._, f32[64,8,128]{2,1,0:T(8,128)S(1)} %get-tuple-element.80.strip_ref, bf16[64,8,128]{2,1,0:T(8,128)(2,1)S(1)} %collective-permute-done.halo_ref), custom_call_target="tpu_custom_call", output_to_operand_aliasing={{}: (0, {})} | custom-call | tf_op jit(solution)/shard_map/pallas_call | solution.py:428
Async XLA Ops:
  27.0 4.6 %collective-permute-start = (bf16[64,8,128]{2,1,0:T(8,128)(2,1)}, bf16[64,8,128]{2,1,0:T(8,128)(2,1)S(1)}, u32[]{:S(2)}, u32[]{:S(2)}) collective-permute-start(bf16[64,8,128]{2,1,0:T(8,128)(2,1)} %get-tuple-element.81), channel_id=1, source_target_pairs={{0,32},{32,64},{64,96},{96,128},{128,160},{160,192},{192,224},{224... | collective-permute-start | bytes 393224 | tf_op jit(solution)/shard_map/ppermute | solution.py:459

commit v6 on v5

--- a/solution.py
+++ b/solution.py
@@ -45,16 +45,24 @@
     edge = member & (u % GU > GU - TAPS)
     plain_f = (member & jnp.logical_not(edge)).astype(F32)
     edge_f = edge.astype(F32)
-    before = lax.broadcasted_iota(jnp.int32, (rows, rows), 0) < lax.broadcasted_iota(
-        jnp.int32, (rows, rows), 1
+    flags = jnp.concatenate([edge_f, plain_f], axis=0)
+    blocks = [flags[:, at : at + LANES] for at in range(0, rows, LANES)]
+    before = lax.broadcasted_iota(jnp.int32, (LANES, LANES), 0) < lax.broadcasted_iota(
+        jnp.int32, (LANES, LANES), 1
     )
-    rank = jnp.dot(
-        jnp.concatenate([edge_f, plain_f], axis=0).astype(BF16),
+    inside = jnp.dot(
+        jnp.concatenate(blocks, axis=0).astype(BF16),
         before.astype(F32).astype(BF16),
         preferred_element_type=F32,
     )
-    edges = jnp.sum(edge_f, axis=1, keepdims=True)
-    total = edges + jnp.sum(plain_f, axis=1, keepdims=True)
+    seen = jnp.zeros((2 * n_dst, 1), F32)
+    ranks = []
+    for b, block_flags in enumerate(blocks):
+        ranks.append(inside[2 * n_dst * b : 2 * n_dst * (b + 1)] + seen)
+        seen = seen + jnp.sum(block_flags, axis=1, keepdims=True)
+    rank = jnp.concatenate(ranks, axis=1)
+    edges = seen[:n_dst]
+    total = edges + seen[n_dst:]
     rank = jnp.where(edge, rank[:n_dst], rank[n_dst:] + edges)
     rank = jnp.where(member, rank.astype(jnp.int32), -1)
     over = (jnp.max(total, axis=0, keepdims=True) > cap).astype(F32)
@@ -88,8 +96,14 @@
         axis=0,
     )
     slot = lax.broadcasted_iota(jnp.int32, (cap, rows), 0)
+    exact = cap <= 256
+    if exact:
+        slot = slot.astype(F32).astype(BF16)
+        rank = rank.astype(F32).astype(BF16)
+    one, nought = jnp.ones((), BF16), jnp.zeros((), BF16)
     for d in range(n_dst):
-        pick = (slot == rank[d : d + 1, :]).astype(F32).astype(BF16)
+        same = slot == rank[d : d + 1, :]
+        pick = jnp.where(same, one, nought) if exact else same.astype(F32).astype(BF16)
         picks_s[d * half : (d + 1) * half, :rows] = pick[:half]
         picks_s[d * half : (d + 1) * half, rows:] = pick[half:]
     sent = lax.dot_general(picks_s[...], source, NT, preferred_element_type=F32)
@@ -387,7 +401,7 @@
         copy_out(i).wait()
 
 
-def main(half, msgs, held, other, tables, step_chans=16):
+def main(half, msgs, held, other, tables, step_chans=8):
     depth, width = other.shape
     chans = depth - META
     vmem = pl.BlockSpec(memory_space=pltpu.VMEM)

time: 32.7 us -> 32.7 us (level)
  transfers between devices with their start and end apart: 1 -> 1, of which waited for: 0 -> 1; matrix products, arithmetic and copies ran while one was open for 0% -> 0% of each run, Pallas kernels for 7% -> 7%
where the time goes in v6:
time: 32.7 us; the launch traced here: 32.5 us
  blocking collectives  22.3 us (68%)
  Pallas kernels  6.84 us (21%)
  starting transfers between devices  2.37 us (7%)
  loops' own time  0.65 us (2%)
    all_to_all x1, blocking collectives, exchange(): return (lax.all_to_all(sent, 'fv', 0, 0), tables)  22.3 us
    pallas_call x1, Pallas kernels, border(): pl.pallas_call(functools.partial(usual_kernel if usual else whole_kernel,...  2.49 us
    ppermute x1, starting transfers between devices, per_device(): came = lax.ppermute(halo, 'fu', [(i, (i + 1) % n_fu) for i in range(n_fu)])  2.37 us
    pallas_call x1, Pallas kernels, main(): pl.pallas_call(functools.partial(main_kernel, half, step_chans), out_shap...  2.16 us
    pallas_call x1, Pallas kernels, pack(): pl.pallas_call(functools.partial(pack_kernel, half, n_dst), out_shape=(ja...  1.45 us
    pallas_call x1, Pallas kernels, join(): pl.pallas_call(join_kernel, out_shape=jax.ShapeDtypeStruct(grid.shape, gr...  0.74 us
    another operation x1, loops' own time, per_device(): lax.while_loop(lambda state: state[2][0, 0] > 0, whole, (other, halo, over))  0.65 us
  transfers between devices with their start and end apart: 1, of which 1 were waited for; matrix products, arithmetic and copies ran while one was open for 0% of the time, Pallas kernels for 7%

profile of v6, /device:TPU:1, one launch (start us, length us, event | category | flops | bytes accessed | tf_op | source)
XLA Modules:
  0.0 32.5 jit_solution(7396990717986020530)
XLA Ops:
  0.0 1.4 %shard_map.73 = (bf16[16,48,128]{2,1,0:T(8,128)(2,1)S(1)}, f32[16,16]{1,0:T(8,128)S(1)}) custom-call(s32[1,384]{1,0:T(1,128)} %u_ref.1, s32[1,384]{1,0:T(1,128)} %v_ref.1, s32[1,384]{1,0:T(1,128)} %w_ref.1, s32[1,3]{1,0:T(1,128)} %counts_ref.1, bf16[64,384]{1,0:T(8,128)(2,1)} %bitcast.6, f32[8,16]{1,0:T(8,128)} %bitcast.8, f32[8,16]{1,0:T(8,128)} %bitcast.10), custom_call_target="tpu_custom_call" | custom-call | tf_op jit(solution)/shard_map/pallas_call | solution.py:132
  1.4 22.3 %all_to_all.10.msgs_ref = bf16[16,48,128]{2,1,0:T(8,128)(2,1)S(1)} all-to-all(bf16[16,48,128]{2,1,0:T(8,128)(2,1)S(1)} %get-tuple-element.72), channel_id=1, replica_groups=mesh['fu'=8,'fv'=16,'ch'=2] {'fv'}, dimensions={0} | all-to-all | bytes 393216 | tf_op jit(solution)/shard_map/all_to_all | solution.py:464
  23.8 2.5 %shard_map.74 = (bf16[72,1280]{1,0:T(8,128)(2,1)S(1)}, bf16[64,8,128]{2,1,0:T(8,128)(2,1)}, s32[1,1]{1,0:T(1,128)}, bf16[72,4096]{1,0:T(8,128)(2,1)}) custom-call(bf16[16,48,128]{2,1,0:T(8,128)(2,1)S(1)} %all_to_all.10.msgs_ref, f32[16,16]{1,0:T(8,128)S(1)} %get-tuple-element.125.tables_ref), custom_call_target="tpu_custom_call" | custom-call | tf_op jit(solution)/shard_map/pallas_call | solution.py:292
  26.3 0.7 %while.11 = (bf16[72,4096]{1,0:T(8,128)(2,1)}, bf16[64,8,128]{2,1,0:T(8,128)(2,1)}, s32[1,1]{1,0:T(1,128)}, f32[16,8]{0,1:T(8,128)}, f32[16,8]{0,1:T(8,128)}, /*...) while((bf16[72,4096]{1,0:T(8,128)(2,1)}, ...), condition=%region_1.0_spmd, body=%region_0.0_spmd | while | flops 1 | bytes 1769569 | solution.py:472
  26.9 2.4 %collective-permute-start = (bf16[64,8,128]{2,1,0:T(8,128)(2,1)}, bf16[64,8,128]{2,1,0:T(8,128)(2,1)S(1)}, u32[]{:S(2)}, u32[]{:S(2)}) collective-permute-start(bf16[64,8,128]{2,1,0:T(8,128)(2,1)} %get-tuple-element.81), channel_id=1, source_target_pairs={{0,32},{32,64},{64,96},{96,128},{128,160},{160,192},{192,224},{224... | collective-permute-start | bytes 393224 | tf_op jit(solution)/shard_map/ppermute | solution.py:473
  29.3 2.2 %shard_map.75 = (f32[64,64,128]{2,1,0:T(8,128)}, f32[64,8,128]{2,1,0:T(8,128)S(1)}) custom-call(bf16[16,48,128]{2,1,0:T(8,128)(2,1)S(1)} %all_to_all.10.msgs_ref, bf16[72,1280]{1,0:T(8,128)(2,1)S(1)} %get-tuple-element.74.held_ref, bf16[72,4096]{1,0:T(8,128)(2,1)} %get-tuple-element.78.other_ref, f32[16,16]{1,0:T(8,128)S(1)} %get-tuple-element.149), custom_call_target="tpu_custom_call" | custom-call | tf_op jit(solution)/shard_map/pallas_call | solution.py:408
  31.5 0.1 collective-permute-done.halo_ref
  31.6 0.7 %shard_map.76 = f32[64,64,128]{2,1,0:T(8,128)} custom-call(f32[64,64,128]{2,1,0:T(8,128)} %get-tuple-element.79._, f32[64,8,128]{2,1,0:T(8,128)S(1)} %get-tuple-element.80.strip_ref, bf16[64,8,128]{2,1,0:T(8,128)(2,1)S(1)} %collective-permute-done.halo_ref), custom_call_target="tpu_custom_call", output_to_operand_aliasing={{}: (0, {})} | custom-call | tf_op jit(solution)/shard_map/pallas_call | solution.py:442
Async XLA Ops:
  26.9 4.6 %collective-permute-start = (bf16[64,8,128]{2,1,0:T(8,128)(2,1)}, bf16[64,8,128]{2,1,0:T(8,128)(2,1)S(1)}, u32[]{:S(2)}, u32[]{:S(2)}) collective-permute-start(bf16[64,8,128]{2,1,0:T(8,128)(2,1)} %get-tuple-element.81), channel_id=1, source_target_pairs={{0,32},{32,64},{64,96},{96,128},{128,160},{160,192},{192,224},{224... | collective-permute-start | bytes 393224 | tf_op jit(solution)/shard_map/ppermute | solution.py:473

commit v7 on v5

--- a/solution.py
+++ b/solution.py
@@ -248,9 +248,7 @@
     def emit(total):
         halo_ref[...] = total.reshape(chans, TAPS, GV).astype(BF16)
 
-    @pl.when(chunks <= 1)
-    def _():
-        emit(chunk(0))
+    emit(chunk(0))
 
     @pl.when(chunks > 1)
     def _():

time: 32.7 us -> 32.6 us (level)
  no operation moved by 1% of the time
where the time goes in v7:
time: 32.6 us; the launch traced here: 32.4 us
  blocking collectives  22.3 us (68%)
  Pallas kernels  6.89 us (21%)
  starting transfers between devices  2.36 us (7%)
  loops' own time  0.65 us (2%)
    all_to_all x1, blocking collectives, exchange(): return (lax.all_to_all(sent, 'fv', 0, 0), tables)  22.3 us
    pallas_call x1, Pallas kernels, border(): pl.pallas_call(functools.partial(usual_kernel if usual else whole_kernel,...  2.37 us
    ppermute x1, starting transfers between devices, per_device(): came = lax.ppermute(halo, 'fu', [(i, (i + 1) % n_fu) for i in range(n_fu)])  2.36 us
    pallas_call x1, Pallas kernels, main(): pl.pallas_call(functools.partial(main_kernel, half, step_chans), out_shap...  2.27 us
    pallas_call x1, Pallas kernels, pack(): pl.pallas_call(functools.partial(pack_kernel, half, n_dst), out_shape=(ja...  1.5 us
    pallas_call x1, Pallas kernels, join(): pl.pallas_call(join_kernel, out_shape=jax.ShapeDtypeStruct(grid.shape, gr...  0.75 us
    another operation x1, loops' own time, per_device(): lax.while_loop(lambda state: state[2][0, 0] > 0, whole, (other, halo, over))  0.65 us
  transfers between devices with their start and end apart: 1, of which 0 were waited for; matrix products, arithmetic and copies ran while one was open for 0% of the time, Pallas kernels for 7%

profile of v7, /device:TPU:1, one launch (start us, length us, event | category | flops | bytes accessed | tf_op | source)
XLA Modules:
  0.0 32.4 jit_solution(2297386338295813950)
XLA Ops:
  0.0 1.5 %shard_map.73 = (bf16[16,48,128]{2,1,0:T(8,128)(2,1)S(1)}, f32[16,16]{1,0:T(8,128)S(1)}) custom-call(s32[1,384]{1,0:T(1,128)} %u_ref.1, s32[1,384]{1,0:T(1,128)} %v_ref.1, s32[1,384]{1,0:T(1,128)} %w_ref.1, s32[1,3]{1,0:T(1,128)} %counts_ref.1, bf16[64,384]{1,0:T(8,128)(2,1)} %bitcast.6, f32[8,16]{1,0:T(8,128)} %bitcast.8, f32[8,16]{1,0:T(8,128)} %bitcast.10), custom_call_target="tpu_custom_call" | custom-call | tf_op jit(solution)/shard_map/pallas_call | solution.py:118
  1.5 22.3 %all_to_all.10.msgs_ref = bf16[16,48,128]{2,1,0:T(8,128)(2,1)S(1)} all-to-all(bf16[16,48,128]{2,1,0:T(8,128)(2,1)S(1)} %get-tuple-element.72), channel_id=1, replica_groups=mesh['fu'=8,'fv'=16,'ch'=2] {'fv'}, dimensions={0} | all-to-all | bytes 393216 | tf_op jit(solution)/shard_map/all_to_all | solution.py:448
  23.8 2.4 %shard_map.74 = (bf16[72,1280]{1,0:T(8,128)(2,1)S(1)}, bf16[64,8,128]{2,1,0:T(8,128)(2,1)}, s32[1,1]{1,0:T(1,128)}, bf16[72,4096]{1,0:T(8,128)(2,1)}) custom-call(bf16[16,48,128]{2,1,0:T(8,128)(2,1)S(1)} %all_to_all.10.msgs_ref, f32[16,16]{1,0:T(8,128)S(1)} %get-tuple-element.125.tables_ref), custom_call_target="tpu_custom_call" | custom-call | tf_op jit(solution)/shard_map/pallas_call | solution.py:276
  26.2 0.7 %while.11 = (bf16[72,4096]{1,0:T(8,128)(2,1)}, bf16[64,8,128]{2,1,0:T(8,128)(2,1)}, s32[1,1]{1,0:T(1,128)}, f32[16,8]{0,1:T(8,128)}, f32[16,8]{0,1:T(8,128)}, /*...) while((bf16[72,4096]{1,0:T(8,128)(2,1)}, ...), condition=%region_1.0_spmd, body=%region_0.0_spmd | while | flops 1 | bytes 1769569 | solution.py:456
  26.9 2.4 %collective-permute-start = (bf16[64,8,128]{2,1,0:T(8,128)(2,1)}, bf16[64,8,128]{2,1,0:T(8,128)(2,1)S(1)}, u32[]{:S(2)}, u32[]{:S(2)}) collective-permute-start(bf16[64,8,128]{2,1,0:T(8,128)(2,1)} %get-tuple-element.81), channel_id=1, source_target_pairs={{0,32},{32,64},{64,96},{96,128},{128,160},{160,192},{192,224},{224... | collective-permute-start | bytes 393224 | tf_op jit(solution)/shard_map/ppermute | solution.py:457
  29.2 2.3 %shard_map.75 = (f32[64,64,128]{2,1,0:T(8,128)}, f32[64,8,128]{2,1,0:T(8,128)S(1)}) custom-call(bf16[16,48,128]{2,1,0:T(8,128)(2,1)S(1)} %all_to_all.10.msgs_ref, bf16[72,1280]{1,0:T(8,128)(2,1)S(1)} %get-tuple-element.74.held_ref, bf16[72,4096]{1,0:T(8,128)(2,1)} %get-tuple-element.78.other_ref, f32[16,16]{1,0:T(8,128)S(1)} %get-tuple-element.149), custom_call_target="tpu_custom_call" | custom-call | tf_op jit(solution)/shard_map/pallas_call | solution.py:392
  31.5 0.0 collective-permute-done.halo_ref
  31.5 0.8 %shard_map.76 = f32[64,64,128]{2,1,0:T(8,128)} custom-call(f32[64,64,128]{2,1,0:T(8,128)} %get-tuple-element.79._, f32[64,8,128]{2,1,0:T(8,128)S(1)} %get-tuple-element.80.strip_ref, bf16[64,8,128]{2,1,0:T(8,128)(2,1)S(1)} %collective-permute-done.halo_ref), custom_call_target="tpu_custom_call", output_to_operand_aliasing={{}: (0, {})} | custom-call | tf_op jit(solution)/shard_map/pallas_call | solution.py:426
Async XLA Ops:
  26.9 4.6 %collective-permute-start = (bf16[64,8,128]{2,1,0:T(8,128)(2,1)}, bf16[64,8,128]{2,1,0:T(8,128)(2,1)S(1)}, u32[]{:S(2)}, u32[]{:S(2)}) collective-permute-start(bf16[64,8,128]{2,1,0:T(8,128)(2,1)} %get-tuple-element.81), channel_id=1, source_target_pairs={{0,32},{32,64},{64,96},{96,128},{128,160},{160,192},{192,224},{224... | collective-permute-start | bytes 393224 | tf_op jit(solution)/shard_map/ppermute | solution.py:457
